TPU v7x, 256 devices: a whole 4x4x8 slice. The times are simulated.
256 devices in a mesh: blk: 128 (over z, y_lo, x, core), col: 2 (over y_hi).
Axes of the slice: x: 4, y: 4 (y_hi: 2, y_lo: 2; y = y_hi * 2 + y_lo), z: 8, core: 2. Of those that a mesh axis runs over, the one named last changes fastest.
Arguments:
- tiles: bfloat16 [3072, 128, 128], P('blk'), may hold values from -0.21875 to 0.21875
- tile_rows: int32 [3072], P('blk'), may hold values from 0 to 3, as said below
- tile_cols: int32 [3072], P('blk'), may hold values from 0 to 511, as said below
- tile_count: int32 [128], P('blk'), may hold values from 3 to 24, as said below
- sketch: bfloat16 [65536, 512], P('blk', 'col'), may hold values from -6 to 6
- variant_scale: bfloat16 [65536], P('blk'), may hold values from 0.5 to 2
Outputs:
- basis_rows: float32 [65536, 512], P('blk', 'col')
Inputs may be any that keep to these rules, and one draw needn't show every extreme that they name: `tile_count`: each row group has 24, 12, 6 or 3 live slots, and at least one group has all 24 live. `tile_rows`: no two slots of a row group name the same block row and block column. Slots at or past their group's count are not part of the matrix. `tile_cols`: within one row group, all slots whose block columns lie in the same run of 4 block columns that starts at a multiple of 4 name the same block column.
All inputs are finite; a program needn't handle non-finite values.
Results may differ from a plain program's by a relative error of at most 0.0059.
Values may be sent and summed in bfloat16 or wider, within the bound.
No kernel may reach another device: no remote copies, remote signals or barrier semaphores. Data moves between devices by JAX's collectives and lax.ppermute only.
A program may use at most 128 MiB of HBM per device.

v0:
```python
import jax
import jax.numpy as jnp
from jax import lax
from jax.experimental import pallas as pl
from jax.experimental.pallas import tpu as pltpu
from jax.sharding import Mesh
from jax.sharding import PartitionSpec as P

RB_DEV = 4
GROUPS = ("z", "y", "x", "core")


def spread(rows, axes):
    return lax.all_to_all(rows, axes, split_axis=0, concat_axis=0, tiled=True)


SUB = 8
F32 = jnp.float32


def block_places():
    own = [((0, 0), (0, 1), (1, 1)), ((2, 2), (2, 3), (3, 3))]
    cross = [((0, 2), (1, 2)), ((0, 3), (1, 3))]
    return [place for side in range(2) for place in own[side] + cross[side]]


def eliminate(rows, edge):
    lane = lax.broadcasted_iota(jnp.int32, (SUB, edge), 1)
    sub = lax.broadcasted_iota(jnp.int32, (SUB, edge), 0)
    rows = list(rows)
    last = len(rows)
    for g in range(last):
        base = g * SUB
        inside = (lane >= base) & (lane < base + SUB)
        start = jnp.where(inside, jnp.where(lane - base == sub, 1.0, 0.0), rows[g])
        columns = [jnp.broadcast_to(rows[g][:, base + c : base + c + 1], (SUB, edge)) for c in range(SUB)]
        s = {(a, c): jnp.broadcast_to(columns[c][a : a + 1, :], (SUB, edge)) for a in range(SUB) for c in range(a, SUB)}
        x = [jnp.broadcast_to(start[a : a + 1, :], (SUB, edge)) for a in range(SUB)]
        r, low = [], {}
        ahead = g + 1 < last
        if ahead:
            nxt = rows[g + 1]
            fac = [jnp.broadcast_to(nxt[:, base + c : base + c + 1], (SUB, edge)) for c in range(SUB)]
            nxt = jnp.where(inside, 0.0, nxt)
        for a in range(SUB):
            r.append(lax.rsqrt(s[a, a]))
            for c in range(a + 1, SUB):
                low[c, a] = s[a, c] * r[a]
            for c in range(a + 1, SUB):
                for e in range(c, SUB):
                    s[c, e] = s[c, e] - low[c, a] * low[e, a]
            x[a] = x[a] * r[a]
            if ahead:
                fac[a] = fac[a] * r[a]
                nxt = nxt - fac[a] * x[a]
            for c in range(a + 1, SUB):
                x[c] = x[c] - low[c, a] * x[a]
                if ahead:
                    fac[c] = fac[c] - fac[a] * low[c, a]
        done = x[0]
        for a in range(1, SUB):
            done = jnp.where(sub == a, x[a], done)
        if g + 2 < last:
            z = [None] * SUB
            for a in range(SUB - 1, -1, -1):
                t = x[a]
                for c in range(a + 1, SUB):
                    t = t - low[c, a] * z[c]
                z[a] = t * r[a]
            for h in range(g + 2, last):
                old = rows[h]
                t = jnp.where(inside, 0.0, old)
                for a in range(SUB):
                    t = t - jnp.broadcast_to(old[:, base + a : base + a + 1], (SUB, edge)) * z[a]
                rows[h] = t
        if ahead:
            rows[g + 1] = nxt
        rows[g] = done
    return rows


def factor_body(gram_ref, out_ref, work_ref, row_ref):
    edge = row_ref.shape[0]
    size = out_ref.shape[0]
    count = size // edge
    hi = lax.Precision.HIGHEST
    for n, (i, j) in enumerate(block_places()):
        work_ref[i * edge : (i + 1) * edge, j * edge : (j + 1) * edge] = gram_ref[:, n * edge : (n + 1) * edge]
    for i in range(1, count):
        work_ref[i * edge : (i + 1) * edge, : i * edge] = jnp.zeros((edge, i * edge), F32)

    def stage(k, carry):
        base = pl.multiple_of(k * edge, edge)
        rows = [work_ref[pl.ds(base + SUB * h, SUB), pl.ds(base, edge)] for h in range(edge // SUB)]
        w = jnp.concatenate(eliminate(rows, edge), axis=0)
        r2 = lax.broadcasted_iota(jnp.int32, (edge, edge), 0)
        c2 = lax.broadcasted_iota(jnp.int32, (edge, edge), 1)
        inv = jnp.where(r2 >= c2, w, 0.0)
        row_ref[...] = jnp.dot(inv, work_ref[pl.ds(base, edge), :], precision=hi, preferred_element_type=F32)
        row_ref[:, pl.ds(base, edge)] = inv
        work_ref[pl.ds(base, edge), :] = row_ref[...]

        def below(i, carry):
            at = pl.multiple_of(i * edge, edge)
            work_ref[pl.ds(at, edge), pl.ds(base, edge)] = jnp.zeros((edge, edge), F32)
            work_ref[pl.ds(at, edge), :] -= lax.dot_general(
                row_ref[:, pl.ds(at, edge)], row_ref[...], (((0,), (0,)), ((), ())),
                precision=hi, preferred_element_type=F32)
            return carry

        return lax.fori_loop(k + 1, count, below, carry)

    lax.fori_loop(0, count, stage, 0)
    out_ref[...] = work_ref[...]
    for i in range(count):
        if i + 1 < count:
            out_ref[i * edge : (i + 1) * edge, (i + 1) * edge :] = jnp.zeros((edge, size - (i + 1) * edge), F32)


def invert_factor(packed, size):
    edge = packed.shape[0]
    return pl.pallas_call(
        factor_body,
        out_shape=jax.ShapeDtypeStruct((size, size), F32),
        scratch_shapes=[pltpu.VMEM((size, size), F32), pltpu.VMEM((edge, size), F32)],
    )(packed)


def gram_body(side_ref, mine_ref, other_ref, packed_ref):
    edge = packed_ref.shape[0]
    first = side_ref[0] == 0
    mine = mine_ref[...]
    other = other_ref[...]
    left = jnp.where(first, mine, other)
    right = jnp.where(first, other[:, :edge], mine[:, edge:])

    def product(a, b):
        return lax.dot_general(a, b, (((0,), (0,)), ((), ())), preferred_element_type=F32)

    own = product(mine, mine)
    cross = product(left, right)
    pieces = (own[:edge, :edge], own[:edge, edge:], own[edge:, edge:], cross[:edge], cross[edge:])
    for n, piece in enumerate(pieces):
        packed_ref[:, n * edge : (n + 1) * edge] = piece


def pair_gram(side, mine, other, edge):
    return pl.pallas_call(
        gram_body,
        out_shape=jax.ShapeDtypeStruct((edge, 5 * edge), F32),
        in_specs=[pl.BlockSpec(memory_space=pltpu.SMEM)] + [pl.BlockSpec(memory_space=pltpu.VMEM)] * 2,
        out_specs=pl.BlockSpec(memory_space=pltpu.VMEM),
    )(side, mine, other)


def local(tiles, tile_rows, tile_cols, tile_count, sketch, variant_scale):
    slots, edge, _ = tiles.shape
    width = sketch.shape[1]
    owners = lax.axis_size(GROUPS)
    cols = lax.axis_size("col")
    own_blocks = sketch.shape[0] // edge
    blocks = owners * own_blocks
    bf16, f32 = jnp.bfloat16, jnp.float32

    own_rows = jnp.swapaxes(sketch.reshape(own_blocks, edge, width), 0, 1)
    own_scales = variant_scale.reshape(own_blocks, edge).T
    live = jnp.arange(slots, dtype=jnp.int32) < tile_count[0]
    run = jnp.where(live, tile_cols // own_blocks, -1).astype(bf16)
    member = (tile_cols % own_blocks).astype(bf16)
    notes = jnp.concatenate([run, member])
    notes = jnp.concatenate([own_scales, jnp.broadcast_to(notes, (edge, 2 * slots))], axis=1)
    notes = jnp.pad(notes, ((0, 0), (0, width - notes.shape[1])))
    packed = jnp.concatenate([own_rows, notes[:, None, :]], axis=1)
    kept = spread(packed, GROUPS)
    kept_rows = kept[:, :own_blocks, :].reshape(blocks, width)
    kept_notes = kept[:, own_blocks, :].astype(f32)
    kept_scale = kept_notes[:, :own_blocks].reshape(blocks, 1)
    all_runs = kept_notes[:, own_blocks : own_blocks + slots]
    all_members = kept_notes[:, own_blocks + slots : own_blocks + 2 * slots]
    all_cols = (all_runs * own_blocks + all_members).astype(jnp.int32)
    block_ids = jnp.arange(blocks, dtype=jnp.int32)
    picks = (all_cols[:, :, None] == block_ids).astype(bf16).reshape(owners * slots, blocks)

    row_ids = jnp.arange(RB_DEV, dtype=jnp.int32)
    row_mask = (tile_rows[:, None] == row_ids).astype(bf16)
    turned = jnp.transpose(tiles, (2, 0, 1))
    wide = turned[:, :, None, :] * row_mask[None, :, :, None]
    wide = wide.reshape(edge * slots, RB_DEV * edge)

    def forward(kept_operand):
        sent = jnp.dot(picks, kept_operand, preferred_element_type=f32).astype(bf16)
        fetched = spread(sent.reshape(owners, slots, width), GROUPS).reshape(edge * slots, width)
        return lax.dot_general(
            wide, fetched, (((0,), (0,)), ((), ())), preferred_element_type=f32
        ).astype(bf16)

    scaled = (kept_scale * kept_rows.astype(f32)).astype(bf16)
    range_rows = lax.optimization_barrier(forward(scaled))
    terms = jnp.dot(wide, range_rows, preferred_element_type=f32).astype(bf16)
    arrived = spread(terms.reshape(owners, slots, width), GROUPS).reshape(owners * slots, width)
    back = lax.dot_general(picks, arrived, (((0,), (0,)), ((), ())), preferred_element_type=f32)
    weighted = ((kept_scale * kept_scale) * back).astype(bf16)
    power_rows = forward(lax.optimization_barrier(weighted))

    side = lax.axis_index("col")
    other = lax.ppermute(power_rows, "col", [(0, 1), (1, 0)])
    packed_gram = pair_gram(side.reshape(1), power_rows, other, edge)
    left = jnp.where(side == 0, power_rows, other)
    right = jnp.where(side == 0, other, power_rows)
    all_rows = jnp.concatenate([left, right], axis=1)
    total_rows = all_rows.shape[0] * owners
    share = spread(packed_gram.reshape(owners, 1, -1), GROUPS).sum(0) / total_rows
    summed = spread(jnp.broadcast_to(share, (owners * cols,) + share.shape), GROUPS + ("col",))
    inverse = invert_factor(summed.reshape(owners, -1), width * cols)
    own_inverse = lax.dynamic_slice_in_dim(inverse, side * width, width, 0)
    return jnp.dot(all_rows.astype(f32), own_inverse.T, precision=lax.Precision.HIGHEST)


def solution(mesh):
    owners, cols = mesh.devices.shape
    fine = Mesh(mesh.devices.reshape(owners // 16, 2, 4, 2, cols), GROUPS + ("col",))
    grouped = P(GROUPS)
    placed = (P(GROUPS, None, None), grouped, grouped, grouped, P(GROUPS, "col"), grouped)
    return jax.shard_map(
        local, mesh=fine, in_specs=placed, out_specs=P(GROUPS, "col"), check_vma=False
    )
```

profile of v0, /device:TPU:1, one launch (start us, length us, event | category | flops | bytes accessed | tf_op | source)
XLA Modules:
  0.0 290.4 jit_solution(17501588989090237430)
XLA Ops:
  0.7 0.7 fusion.33
  1.4 0.8 pad_maximum_fusion.1
  2.4 1.2 copy.45
  3.6 0.3 pad_maximum_fusion
  3.8 33.7 %all_to_all.30 = bf16[128,5,256]{2,1,0:T(8,128)(2,1)S(1)} all-to-all(bf16[128,5,256]{2,1,0:T(8,128)(2,1)S(1)} %pad_maximum_fusion), channel_id=1, replica_groups=mesh['z'=8,'y'=2,'x'=4,'core'=2,'col'=2] {'z','y','x','core'}, dimensions={0} | all-to-all | bytes 655360 | tf_op jit(solution)/shard_map/all_to_all | solution.py:14
  38.3 2.6 fusion.3
  41.0 6.6 %all-to-all-start.1 = ((bf16[128,24,256]{2,1,0:T(8,128)(2,1)}), bf16[128,24,256]{2,1,0:T(8,128)(2,1)}, u32[]{:S(2)}, u32[]{:S(2)}) async-start(bf16[128,24,256]{2,1,0:T(8,128)(2,1)} %bitcast.7), calls=%async_computation.1 | async-start | bytes 3145728 | tf_op jit(solution)/shard_map/all_to_all | solution.py:14
  47.5 1.3 copy.18
  48.9 2.8 broadcast_multiply_fusion
  51.7 35.6 %all-to-all-done.1 = bf16[128,24,256]{2,1,0:T(8,128)(2,1)} async-done(((bf16[128,24,256]{2,1,0:T(8,128)(2,1)}), bf16[128,24,256]{2,1,0:T(8,128)(2,1)}, u32[]{:S(2)}, u32[]{:S(2)}) %all-to-all-start.1) | async-done | bytes 1572896 | tf_op jit(solution)/shard_map/all_to_all | solution.py:14
  87.3 2.4 fusion.19
  89.8 2.1 convolution_convert_fusion
  91.9 7.7 %all-to-all-start.2 = ((bf16[128,24,256]{2,1,0:T(8,128)(2,1)}), bf16[128,24,256]{2,1,0:T(8,128)(2,1)}, u32[]{:S(2)}, u32[]{:S(2)}) async-start(bf16[128,24,256]{2,1,0:T(8,128)(2,1)} %bitcast.49), calls=%async_computation.2 | async-start | bytes 3145728 | tf_op jit(solution)/shard_map/all_to_all | solution.py:14
  99.6 39.7 %all-to-all-done.2 = bf16[128,24,256]{2,1,0:T(8,128)(2,1)} async-done(((bf16[128,24,256]{2,1,0:T(8,128)(2,1)}), bf16[128,24,256]{2,1,0:T(8,128)(2,1)}, u32[]{:S(2)}, u32[]{:S(2)}) %all-to-all-start.2) | async-done | bytes 1572896 | tf_op jit(solution)/shard_map/all_to_all | solution.py:14
  139.3 3.7 %fusion.18 = bf16[512,256]{1,0:T(8,128)(2,1)S(1)} fusion(bf16[128,24,256]{2,1,0:T(8,128)(2,1)} %all-to-all-done.2, s32[128,24]{1,0:T(8,128)S(1)} %fusion.31, f32[512]{0:T(512)S(1)} %mul.67), kind=kOutput, calls=%fused_computation.22 | convolution fusion | flops 807141376 | bytes 1849344 | tf_op jit(solution)/shard_map/dot_general | solution.py:201
  142.9 1.7 fusion.4
  144.6 47.0 %all_to_all.31 = bf16[128,24,256]{2,1,0:T(8,128)(2,1)S(1)} all-to-all(bf16[128,24,256]{2,1,0:T(8,128)(2,1)S(1)} %bitcast.50), channel_id=1, replica_groups=mesh['z'=8,'y'=2,'x'=4,'core'=2,'col'=2] {'z','y','x','core'}, dimensions={0} | all-to-all | bytes 3145728 | tf_op jit(solution)/shard_map/all_to_all | solution.py:14
  191.7 1.1 fusion.22.mine_ref
  192.8 2.7 collective-permute-start
  195.5 6.4 %collective-permute-done.other_ref = bf16[512,256]{1,0:T(8,128)(2,1)S(1)} collective-permute-done((bf16[512,256]{1,0:T(8,128)(2,1)S(1)}, bf16[512,256]{1,0:T(8,128)(2,1)S(1)}, u32[]{:S(2)}, u32[]{:S(2)}) %collective-permute-start) | collective-permute-done | bytes 262176 | tf_op jit(solution)/shard_map/ppermute | solution.py:206
  201.8 0.7 copy-done.2
  202.5 2.1 shard_map.64
  204.6 1.4 copy.23
  206.0 23.3 %all_to_all.32 = f32[128,1,640]{2,1,0:T(1,128)S(1)} all-to-all(f32[128,1,640]{2,1,0:T(1,128)S(1)} %copy.23), channel_id=1, replica_groups=mesh['z'=8,'y'=2,'x'=4,'core'=2,'col'=2] {'z','y','x','core'}, dimensions={0} | all-to-all | bytes 655360 | tf_op jit(solution)/shard_map/all_to_all | solution.py:14
  229.3 0.2 reduce_sum.9
  229.5 1.2 broadcast_in_dim.10
  230.7 6.7 %all-to-all-start.5 = ((f32[256,1,640]{2,1,0:T(1,128)}), f32[256,1,640]{2,1,0:T(1,128)S(1)}, u32[]{:S(2)}, u32[]{:S(2)}) async-start(f32[256,1,640]{2,1,0:T(1,128)} %broadcast_in_dim.10), calls=%async_computation.5 | async-start | bytes 1310720 | tf_op jit(solution)/shard_map/all_to_all | solution.py:14
  237.5 23.4 %all-to-all-done.5 = f32[256,1,640]{2,1,0:T(1,128)S(1)} async-done(((f32[256,1,640]{2,1,0:T(1,128)}), f32[256,1,640]{2,1,0:T(1,128)S(1)}, u32[]{:S(2)}, u32[]{:S(2)}) %all-to-all-start.5) | async-done | bytes 655392 | tf_op jit(solution)/shard_map/all_to_all | solution.py:14
  260.9 1.6 reduce.1
  262.4 1.1 reshape.108.gram_ref
  263.5 24.4 %shard_map.65 = f32[512,512]{1,0:T(8,128)} custom-call(f32[128,1280]{1,0:T(8,128)} %reshape.108.gram_ref), custom_call_target="tpu_custom_call" | custom-call | tf_op jit(solution)/shard_map/pallas_call | solution.py:122
  287.9 2.5 fusion.25
  (27 shorter events, 1.2 us)
Async XLA Ops:
  41.0 6.6 %copy-start.4 = (bf16[24,128,128]{2,1,0:T(8,128)(2,1)S(1)}, bf16[24,128,128]{2,1,0:T(8,128)(2,1)}, u32[]{:S(2)}) copy-start(bf16[24,128,128]{2,1,0:T(8,128)(2,1)} %param.6) | copy-start | bytes 2359300
  41.0 7.9 %copy-start.5 = (s32[24]{0:T(128)S(1)}, s32[24]{0:T(128)}, u32[]{:S(2)}) copy-start(s32[24]{0:T(128)} %param.7) | copy-start | bytes 292
  41.0 46.4 %all-to-all-start.1 = ((bf16[128,24,256]{2,1,0:T(8,128)(2,1)}), bf16[128,24,256]{2,1,0:T(8,128)(2,1)}, u32[]{:S(2)}, u32[]{:S(2)}) async-start(bf16[128,24,256]{2,1,0:T(8,128)(2,1)} %bitcast.7), calls=%async_computation.1 | async-start | bytes 3145728 | tf_op jit(solution)/shard_map/all_to_all | solution.py:14
  91.9 47.4 %all-to-all-start.2 = ((bf16[128,24,256]{2,1,0:T(8,128)(2,1)}), bf16[128,24,256]{2,1,0:T(8,128)(2,1)}, u32[]{:S(2)}, u32[]{:S(2)}) async-start(bf16[128,24,256]{2,1,0:T(8,128)(2,1)} %bitcast.49), calls=%async_computation.2 | async-start | bytes 3145728 | tf_op jit(solution)/shard_map/all_to_all | solution.py:14
  192.7 9.1 %copy-start = (bf16[512,256]{1,0:T(8,128)(2,1)}, bf16[512,256]{1,0:T(8,128)(2,1)S(1)}, u32[]{:S(2)}) copy-start(bf16[512,256]{1,0:T(8,128)(2,1)S(1)} %fusion.22.mine_ref) | copy-start | bytes 786436
  192.8 9.1 %collective-permute-start = (bf16[512,256]{1,0:T(8,128)(2,1)S(1)}, bf16[512,256]{1,0:T(8,128)(2,1)S(1)}, u32[]{:S(2)}, u32[]{:S(2)}) collective-permute-start(bf16[512,256]{1,0:T(8,128)(2,1)S(1)} %fusion.22.mine_ref), channel_id=1, source_target_pairs={{0,1},{1,0},{2,3},{3,2},{4,5},{5,4},{6,7},{7,6},{8,9},{9,8},{10,11... | collective-permute-start | bytes 786440 | tf_op jit(solution)/shard_map/ppermute | solution.py:206
  201.8 0.7 copy-start.2
  204.6 32.8 %copy-start.1 = (bf16[512,256]{1,0:T(8,128)(2,1)S(1)}, bf16[512,256]{1,0:T(8,128)(2,1)}, u32[]{:S(2)}) copy-start(bf16[512,256]{1,0:T(8,128)(2,1)} %copy-done) | copy-start | bytes 786436
  204.6 32.8 %copy-start.3 = (bf16[512,256]{1,0:T(8,128)(2,1)S(1)}, bf16[512,256]{1,0:T(8,128)(2,1)}, u32[]{:S(2)}) copy-start(bf16[512,256]{1,0:T(8,128)(2,1)} %copy-done.2) | copy-start | bytes 786436
  230.7 30.2 %all-to-all-start.5 = ((f32[256,1,640]{2,1,0:T(1,128)}), f32[256,1,640]{2,1,0:T(1,128)S(1)}, u32[]{:S(2)}, u32[]{:S(2)}) async-start(f32[256,1,640]{2,1,0:T(1,128)} %broadcast_in_dim.10), calls=%async_computation.5 | async-start | bytes 1310720 | tf_op jit(solution)/shard_map/all_to_all | solution.py:14
where the time goes:
time: 291 us; the launch traced here: 290 us
  waiting for transfers between devices  105 us (36%)
  blocking collectives  104 us (36%)
  Pallas kernels  26.5 us (9%)
  starting transfers between devices  23.7 us (8%)
  matrix products  16.1 us (6%)
  local copies, waits for them, and re-layouts  7.4 us (3%)
  other arithmetic  6.8 us (2%)
    all_to_all x3, blocking collectives, spread(): return lax.all_to_all(rows, axes, split_axis=0, concat_axis=0, tiled=True)  104 us
    all_to_all x3, waiting for transfers between devices, spread(): return lax.all_to_all(rows, axes, split_axis=0, concat_axis=0, tiled=True)  98.7 us
    pallas_call x1, Pallas kernels, invert_factor(): pl.pallas_call(factor_body, out_shape=jax.ShapeDtypeStruct((size, size),...  24.4 us
    all_to_all x3, starting transfers between devices, spread(): return lax.all_to_all(rows, axes, split_axis=0, concat_axis=0, tiled=True)  20.9 us
    ppermute x1, waiting for transfers between devices, local(): other = lax.ppermute(power_rows, 'col', [(0, 1), (1, 0)])  6.35 us
  transfers between devices with their start and end apart: 4, of which 4 were waited for; matrix products, arithmetic and copies ran while one was open for 1% of the time, Pallas kernels for 0%

commit v1 on v0

--- a/solution.py
+++ b/solution.py
@@ -7,7 +7,8 @@
 from jax.sharding import PartitionSpec as P
 
 RB_DEV = 4
-GROUPS = ("z", "y", "x", "core")
+CHIPS = ("z", "y", "x")
+GROUPS = CHIPS + ("core",)
 
 
 def spread(rows, axes):
@@ -79,13 +80,17 @@
     return rows
 
 
-def factor_body(gram_ref, out_ref, work_ref, row_ref):
-    edge = row_ref.shape[0]
-    size = out_ref.shape[0]
+def basis_body(ids_ref, own_ref, twin_ref, mine_ref, other_ref, out_ref, work_ref, row_ref, mix_ref):
+    edge, size = row_ref.shape
     count = size // edge
     hi = lax.Precision.HIGHEST
+    part = own_ref.shape[0]
+    core = ids_ref[1]
     for n, (i, j) in enumerate(block_places()):
-        work_ref[i * edge : (i + 1) * edge, j * edge : (j + 1) * edge] = gram_ref[:, n * edge : (n + 1) * edge]
+        lanes = slice(n * edge, (n + 1) * edge)
+        mix_ref[pl.ds(n * edge + core, part, 2), :] = own_ref[:, lanes]
+        mix_ref[pl.ds(n * edge + 1 - core, part, 2), :] = twin_ref[:, lanes]
+        work_ref[i * edge : (i + 1) * edge, j * edge : (j + 1) * edge] = mix_ref[n * edge : (n + 1) * edge, :]
     for i in range(1, count):
         work_ref[i * edge : (i + 1) * edge, : i * edge] = jnp.zeros((edge, i * edge), F32)
 
@@ -111,19 +116,33 @@
         return lax.fori_loop(k + 1, count, below, carry)
 
     lax.fori_loop(0, count, stage, 0)
-    out_ref[...] = work_ref[...]
-    for i in range(count):
-        if i + 1 < count:
-            out_ref[i * edge : (i + 1) * edge, (i + 1) * edge :] = jnp.zeros((edge, size - (i + 1) * edge), F32)
-
-
-def invert_factor(packed, size):
-    edge = packed.shape[0]
+    for i in range(count - 1):
+        work_ref[i * edge : (i + 1) * edge, (i + 1) * edge :] = jnp.zeros((edge, size - (i + 1) * edge), F32)
+    width = mine_ref.shape[1]
+    first = ids_ref[0] == 0
+    left = jnp.where(first, mine_ref[...], other_ref[...])
+    right = jnp.where(first, other_ref[...], mine_ref[...])
+    rest = work_ref[pl.ds(pl.multiple_of(ids_ref[0] * width, width), width), :]
+    total = jnp.zeros(out_ref.shape, F32)
+    for _ in range(3):
+        step = rest.astype(jnp.bfloat16)
+        rest = rest - step.astype(F32)
+        for at, rows in ((0, left), (width, right)):
+            total += lax.dot_general(
+                rows, step[:, at : at + width], (((1,), (1,)), ((), ())), preferred_element_type=F32
+            )
+    out_ref[...] = total
+
+
+def basis(ids, own, twin, mine, other):
+    edge, size = 2 * own.shape[0], 2 * mine.shape[1]
     return pl.pallas_call(
-        factor_body,
-        out_shape=jax.ShapeDtypeStruct((size, size), F32),
-        scratch_shapes=[pltpu.VMEM((size, size), F32), pltpu.VMEM((edge, size), F32)],
-    )(packed)
+        basis_body,
+        out_shape=jax.ShapeDtypeStruct(mine.shape, F32),
+        in_specs=[pl.BlockSpec(memory_space=pltpu.SMEM)] + [pl.BlockSpec(memory_space=pltpu.VMEM)] * 4,
+        out_specs=pl.BlockSpec(memory_space=pltpu.VMEM),
+        scratch_shapes=[pltpu.VMEM((size, size), F32), pltpu.VMEM((edge, size), F32), pltpu.VMEM((own.size // edge * 2, edge), F32)],
+    )(ids, own, twin, mine, other)
 
 
 def gram_body(side_ref, mine_ref, other_ref, packed_ref):
@@ -170,10 +189,13 @@
     notes = jnp.concatenate([run, member])
     notes = jnp.concatenate([own_scales, jnp.broadcast_to(notes, (edge, 2 * slots))], axis=1)
     notes = jnp.pad(notes, ((0, 0), (0, width - notes.shape[1])))
-    packed = jnp.concatenate([own_rows, notes[:, None, :]], axis=1)
+    packed = jnp.concatenate(
+        [own_rows.reshape(edge, 2, -1), notes.reshape(edge, 2, -1)], axis=2
+    )
     kept = spread(packed, GROUPS)
-    kept_rows = kept[:, :own_blocks, :].reshape(blocks, width)
-    kept_notes = kept[:, own_blocks, :].astype(f32)
+    row_part = own_blocks // 2 * width
+    kept_rows = kept[:, :, :row_part].reshape(blocks, width)
+    kept_notes = kept[:, :, row_part:].reshape(owners, width).astype(f32)
     kept_scale = kept_notes[:, :own_blocks].reshape(blocks, 1)
     all_runs = kept_notes[:, own_blocks : own_blocks + slots]
     all_members = kept_notes[:, own_blocks + slots : own_blocks + 2 * slots]
@@ -205,15 +227,13 @@
     side = lax.axis_index("col")
     other = lax.ppermute(power_rows, "col", [(0, 1), (1, 0)])
     packed_gram = pair_gram(side.reshape(1), power_rows, other, edge)
-    left = jnp.where(side == 0, power_rows, other)
-    right = jnp.where(side == 0, other, power_rows)
-    all_rows = jnp.concatenate([left, right], axis=1)
-    total_rows = all_rows.shape[0] * owners
+    total_rows = power_rows.shape[0] * owners
     share = spread(packed_gram.reshape(owners, 1, -1), GROUPS).sum(0) / total_rows
-    summed = spread(jnp.broadcast_to(share, (owners * cols,) + share.shape), GROUPS + ("col",))
-    inverse = invert_factor(summed.reshape(owners, -1), width * cols)
-    own_inverse = lax.dynamic_slice_in_dim(inverse, side * width, width, 0)
-    return jnp.dot(all_rows.astype(f32), own_inverse.T, precision=lax.Precision.HIGHEST)
+    own = spread(jnp.broadcast_to(share, (owners,) + share.shape), CHIPS + ("col",))
+    twin = lax.ppermute(own, "core", [(0, 1), (1, 0)])
+    ids = jnp.stack([side, lax.axis_index("core")])
+    half = (owners // 2, -1)
+    return basis(ids, own.reshape(half), twin.reshape(half), power_rows, other)
 
 
 def solution(mesh):

time: 291 us -> 279 us (0.959)
  waiting for transfers between devices: 105 us -> 81.5 us
  blocking collectives: 104 us -> 120 us
  starting transfers between devices: 23.7 us -> 20.3 us
    all_to_all x3 -> x2, waiting for transfers between devices: 98.7 us -> 75.1 us  [spread(): return lax.all_to_all(rows, axes, split_axis=0, concat_axis=0, tiled=True)]
    all_to_all x3 -> x4, blocking collectives: 104 us -> 120 us  [spread(): return lax.all_to_all(rows, axes, split_axis=0, concat_axis=0, tiled=True)]
    all_to_all x3 -> x2, starting transfers between devices: 20.9 us -> 14.2 us  [spread(): return lax.all_to_all(rows, axes, split_axis=0, concat_axis=0, tiled=True)]
    ppermute x0 -> x1, starting transfers between devices: none -> 3.44 us  [local(): twin = lax.ppermute(own, 'core', [(0, 1), (1, 0)])]
  transfers between devices with their start and end apart: 4 -> 4, of which waited for: 4 -> 3; matrix products, arithmetic and copies ran while one was open for 1% -> 2% of each run, Pallas kernels for 0% -> 0%
where the time goes in v1:
time: 279 us; the launch traced here: 278 us
  blocking collectives  120 us (43%)
  waiting for transfers between devices  81.5 us (29%)
  Pallas kernels  27.1 us (10%)
  starting transfers between devices  20.3 us (7%)
  matrix products  13.6 us (5%)
  local copies, waits for them, and re-layouts  7.5 us (3%)
  other arithmetic  7.12 us (3%)
    all_to_all x4, blocking collectives, spread(): return lax.all_to_all(rows, axes, split_axis=0, concat_axis=0, tiled=True)  120 us
    all_to_all x2, waiting for transfers between devices, spread(): return lax.all_to_all(rows, axes, split_axis=0, concat_axis=0, tiled=True)  75.1 us
    pallas_call x1, Pallas kernels, basis(): pl.pallas_call(basis_body, out_shape=jax.ShapeDtypeStruct(mine.shape, F32...  25 us
    all_to_all x2, starting transfers between devices, spread(): return lax.all_to_all(rows, axes, split_axis=0, concat_axis=0, tiled=True)  14.2 us
    ppermute x1, waiting for transfers between devices, local(): other = lax.ppermute(power_rows, 'col', [(0, 1), (1, 0)])  6.36 us
  transfers between devices with their start and end apart: 4, of which 3 were waited for; matrix products, arithmetic and copies ran while one was open for 2% of the time, Pallas kernels for 0%

profile of v1, /device:TPU:1, one launch (start us, length us, event | category | flops | bytes accessed | tf_op | source)
XLA Modules:
  0.0 278.3 jit_solution(9559337428522588249)
XLA Ops:
  0.7 1.1 copy.19
  1.8 0.7 fusion.28
  2.5 0.8 pad_maximum_fusion.1
  3.3 0.7 copy.20
  4.0 30.3 %all_to_all.30 = bf16[128,2,640]{2,1,0:T(2,128)(2,1)S(1)} all-to-all(bf16[128,2,640]{2,1,0:T(2,128)(2,1)S(1)} %copy.20), channel_id=1, replica_groups=mesh['z'=8,'y'=2,'x'=4,'core'=2,'col'=2] {'z','y','x','core'}, dimensions={0} | all-to-all | bytes 655360 | tf_op jit(solution)/shard_map/all_to_all | solution.py:15
  35.3 2.6 fusion.3
  37.9 6.5 %all-to-all-start.1 = ((bf16[128,24,256]{2,1,0:T(8,128)(2,1)}), bf16[128,24,256]{2,1,0:T(8,128)(2,1)}, u32[]{:S(2)}, u32[]{:S(2)}) async-start(bf16[128,24,256]{2,1,0:T(8,128)(2,1)} %bitcast.10), calls=%async_computation.1 | async-start | bytes 3145728 | tf_op jit(solution)/shard_map/all_to_all | solution.py:15
  44.5 1.3 copy.18
  45.8 2.8 %broadcast_multiply_fusion = bf16[128,24,4,128]{3,2,1,0:T(4,128)(2,1)S(1)} fusion(bf16[24,4]{1,0:T(8,128)(2,1)S(1)} %fusion.27, bf16[128,24,128]{2,1,0:T(8,128)(2,1)} %copy.18), kind=kLoop, calls=%fused_computation.19 | loop fusion | flops 1572864 | bytes 3932352 | tf_op jit(solution)/shard_map/mul | solution.py:209
  48.6 35.4 %all-to-all-done.1 = bf16[128,24,256]{2,1,0:T(8,128)(2,1)} async-done(((bf16[128,24,256]{2,1,0:T(8,128)(2,1)}), bf16[128,24,256]{2,1,0:T(8,128)(2,1)}, u32[]{:S(2)}, u32[]{:S(2)}) %all-to-all-start.1) | async-done | bytes 1572896 | tf_op jit(solution)/shard_map/all_to_all | solution.py:15
  84.0 2.4 fusion.19
  86.4 2.1 convolution_convert_fusion
  88.6 7.7 %all-to-all-start.2 = ((bf16[128,24,256]{2,1,0:T(8,128)(2,1)}), bf16[128,24,256]{2,1,0:T(8,128)(2,1)}, u32[]{:S(2)}, u32[]{:S(2)}) async-start(bf16[128,24,256]{2,1,0:T(8,128)(2,1)} %bitcast.50), calls=%async_computation.2 | async-start | bytes 3145728 | tf_op jit(solution)/shard_map/all_to_all | solution.py:15
  96.3 39.7 %all-to-all-done.2 = bf16[128,24,256]{2,1,0:T(8,128)(2,1)} async-done(((bf16[128,24,256]{2,1,0:T(8,128)(2,1)}), bf16[128,24,256]{2,1,0:T(8,128)(2,1)}, u32[]{:S(2)}, u32[]{:S(2)}) %all-to-all-start.2) | async-done | bytes 1572896 | tf_op jit(solution)/shard_map/all_to_all | solution.py:15
  136.0 3.7 %fusion.18 = bf16[512,256]{1,0:T(8,128)(2,1)S(1)} fusion(bf16[128,24,256]{2,1,0:T(8,128)(2,1)} %all-to-all-done.2, s32[128,24]{1,0:T(8,128)S(1)} %fusion.26, f32[512]{0:T(512)S(1)} %mul.64), kind=kOutput, calls=%fused_computation.22 | convolution fusion | flops 807141376 | bytes 1849344 | tf_op jit(solution)/shard_map/dot_general | solution.py:223
  139.7 1.7 fusion.4
  141.3 47.0 %all_to_all.31 = bf16[128,24,256]{2,1,0:T(8,128)(2,1)S(1)} all-to-all(bf16[128,24,256]{2,1,0:T(8,128)(2,1)S(1)} %bitcast.51), channel_id=1, replica_groups=mesh['z'=8,'y'=2,'x'=4,'core'=2,'col'=2] {'z','y','x','core'}, dimensions={0} | all-to-all | bytes 3145728 | tf_op jit(solution)/shard_map/all_to_all | solution.py:15
  188.4 1.1 fusion.22.mine_ref
  189.5 2.7 collective-permute-start
  192.2 6.4 %collective-permute-done.other_ref = bf16[512,256]{1,0:T(8,128)(2,1)S(1)} collective-permute-done((bf16[512,256]{1,0:T(8,128)(2,1)S(1)}, bf16[512,256]{1,0:T(8,128)(2,1)S(1)}, u32[]{:S(2)}, u32[]{:S(2)}) %collective-permute-start) | collective-permute-done | bytes 262176 | tf_op jit(solution)/shard_map/ppermute | solution.py:228
  198.5 0.7 copy-done.1
  199.2 2.1 shard_map.64
  201.3 1.3 copy.21
  202.6 23.3 %all_to_all.32 = f32[128,1,640]{2,1,0:T(1,128)S(1)} all-to-all(f32[128,1,640]{2,1,0:T(1,128)S(1)} %copy.21), channel_id=1, replica_groups=mesh['z'=8,'y'=2,'x'=4,'core'=2,'col'=2] {'z','y','x','core'}, dimensions={0} | all-to-all | bytes 655360 | tf_op jit(solution)/shard_map/all_to_all | solution.py:15
  226.3 19.7 %all_to_all.33 = f32[128,1,640]{2,1,0:T(1,128)S(1)} all-to-all(f32[128,1,640]{2,1,0:T(1,128)S(1)} %broadcast_in_dim.7), channel_id=1, replica_groups=mesh['z'=8,'y'=2,'x'=4,'core'=2,'col'=2] {'z','y','x','col'}, dimensions={0} | all-to-all | bytes 655360 | tf_op jit(solution)/shard_map/all_to_all | solution.py:15
  246.1 3.4 %collective-permute-start.1 = (f32[128,1,640]{2,1,0:T(1,128)S(1)}, f32[128,1,640]{2,1,0:T(1,128)S(1)}, u32[]{:S(2)}, u32[]{:S(2)}) collective-permute-start(f32[128,1,640]{2,1,0:T(1,128)S(1)} %all_to_all.33), channel_id=1, source_target_pairs={{0,2},{2,0},{1,3},{3,1},{4,6},{6,4},{5,7},{7,5},{8,10},{10,8},{9,1... | collective-permute-start | bytes 983048 | tf_op jit(solution)/shard_map/ppermute | solution.py:233
  249.5 0.6 pad_add_fusion.ids_ref
  250.1 0.8 reduce.1
  250.9 0.8 reshape.117.own_ref
  251.7 0.8 reduce.2
  252.5 0.8 reshape.118.twin_ref
  253.3 25.0 %shard_map.65 = f32[512,256]{1,0:T(8,128)} custom-call(s32[2]{0:T(128)} %pad_add_fusion.ids_ref, f32[64,1280]{1,0:T(8,128)} %reshape.117.own_ref, f32[64,1280]{1,0:T(8,128)} %reshape.118.twin_ref, bf16[512,256]{1,0:T(8,128)(2,1)} %copy-done, bf16[512,256]{1,0:T(8,128)(2,1)} %copy-done.1), custom_call_target="tpu_custom_call" | custom-call | tf_op jit(solution)/shard_map/pallas_call | solution.py:139
  (24 shorter events, 1.6 us)
Async XLA Ops:
  37.9 6.5 %copy-start.2 = (bf16[24,128,128]{2,1,0:T(8,128)(2,1)S(1)}, bf16[24,128,128]{2,1,0:T(8,128)(2,1)}, u32[]{:S(2)}) copy-start(bf16[24,128,128]{2,1,0:T(8,128)(2,1)} %param.6) | copy-start | bytes 2359300
  37.9 7.8 %copy-start.3 = (s32[24]{0:T(128)S(1)}, s32[24]{0:T(128)}, u32[]{:S(2)}) copy-start(s32[24]{0:T(128)} %param.7) | copy-start | bytes 292
  37.9 46.1 %all-to-all-start.1 = ((bf16[128,24,256]{2,1,0:T(8,128)(2,1)}), bf16[128,24,256]{2,1,0:T(8,128)(2,1)}, u32[]{:S(2)}, u32[]{:S(2)}) async-start(bf16[128,24,256]{2,1,0:T(8,128)(2,1)} %bitcast.10), calls=%async_computation.1 | async-start | bytes 3145728 | tf_op jit(solution)/shard_map/all_to_all | solution.py:15
  88.6 47.4 %all-to-all-start.2 = ((bf16[128,24,256]{2,1,0:T(8,128)(2,1)}), bf16[128,24,256]{2,1,0:T(8,128)(2,1)}, u32[]{:S(2)}, u32[]{:S(2)}) async-start(bf16[128,24,256]{2,1,0:T(8,128)(2,1)} %bitcast.50), calls=%async_computation.2 | async-start | bytes 3145728 | tf_op jit(solution)/shard_map/all_to_all | solution.py:15
  189.4 9.1 %copy-start = (bf16[512,256]{1,0:T(8,128)(2,1)}, bf16[512,256]{1,0:T(8,128)(2,1)S(1)}, u32[]{:S(2)}) copy-start(bf16[512,256]{1,0:T(8,128)(2,1)S(1)} %fusion.22.mine_ref) | copy-start | bytes 786436
  189.5 9.1 %collective-permute-start = (bf16[512,256]{1,0:T(8,128)(2,1)S(1)}, bf16[512,256]{1,0:T(8,128)(2,1)S(1)}, u32[]{:S(2)}, u32[]{:S(2)}) collective-permute-start(bf16[512,256]{1,0:T(8,128)(2,1)S(1)} %fusion.22.mine_ref), channel_id=1, source_target_pairs={{0,1},{1,0},{2,3},{3,2},{4,5},{5,4},{6,7},{7,6},{8,9},{9,8},{10,11... | collective-permute-start | bytes 786440 | tf_op jit(solution)/shard_map/ppermute | solution.py:228
  198.5 0.7 copy-start.1
  246.1 5.6 %collective-permute-start.1 = (f32[128,1,640]{2,1,0:T(1,128)S(1)}, f32[128,1,640]{2,1,0:T(1,128)S(1)}, u32[]{:S(2)}, u32[]{:S(2)}) collective-permute-start(f32[128,1,640]{2,1,0:T(1,128)S(1)} %all_to_all.33), channel_id=1, source_target_pairs={{0,2},{2,0},{1,3},{3,1},{4,6},{6,4},{5,7},{7,5},{8,10},{10,8},{9,1... | collective-permute-start | bytes 983048 | tf_op jit(solution)/shard_map/ppermute | solution.py:233

commit v2 on v1

--- a/solution.py
+++ b/solution.py
@@ -25,7 +25,12 @@
     return [place for side in range(2) for place in own[side] + cross[side]]
 
 
-def eliminate(rows, edge):
+def pick(v, at):
+    idx = jnp.full(v.shape, at, jnp.int32)
+    return jnp.take_along_axis(v, idx, axis=1, mode='promise_in_bounds')
+
+
+def eliminate(rows, edge, zero):
     lane = lax.broadcasted_iota(jnp.int32, (SUB, edge), 1)
     sub = lax.broadcasted_iota(jnp.int32, (SUB, edge), 0)
     rows = list(rows)
@@ -34,9 +39,9 @@
         base = g * SUB
         inside = (lane >= base) & (lane < base + SUB)
         start = jnp.where(inside, jnp.where(lane - base == sub, 1.0, 0.0), rows[g])
-        columns = [jnp.broadcast_to(rows[g][:, base + c : base + c + 1], (SUB, edge)) for c in range(SUB)]
-        s = {(a, c): jnp.broadcast_to(columns[c][a : a + 1, :], (SUB, edge)) for a in range(SUB) for c in range(a, SUB)}
-        x = [jnp.broadcast_to(start[a : a + 1, :], (SUB, edge)) for a in range(SUB)]
+        wide_rows = [jnp.broadcast_to(rows[g][a : a + 1, :], (SUB, edge)) + zero for a in range(SUB)]
+        s = {(a, c): pick(wide_rows[a], base + c) for a in range(SUB) for c in range(a, SUB)}
+        x = [jnp.where(inside, jnp.where(lane == base + a, 1.0, 0.0), wide_rows[a]) for a in range(SUB)]
         r, low = [], {}
         ahead = g + 1 < last
         if ahead:
@@ -80,49 +85,60 @@
     return rows
 
 
-def basis_body(ids_ref, own_ref, twin_ref, mine_ref, other_ref, out_ref, work_ref, row_ref, mix_ref):
+def basis_body(
+    side_ref, core_ref, own_ref, twin_ref, mine_ref, other_ref, out_ref, work_ref, inv_ref, row_ref, mix_ref, zero_ref
+):
     edge, size = row_ref.shape
     count = size // edge
     hi = lax.Precision.HIGHEST
-    part = own_ref.shape[0]
-    core = ids_ref[1]
-    for n, (i, j) in enumerate(block_places()):
-        lanes = slice(n * edge, (n + 1) * edge)
-        mix_ref[pl.ds(n * edge + core, part, 2), :] = own_ref[:, lanes]
-        mix_ref[pl.ds(n * edge + 1 - core, part, 2), :] = twin_ref[:, lanes]
+    side, core = side_ref[0], core_ref[0]
+    zero_ref[...] = jnp.zeros(zero_ref.shape, F32)
+    places = block_places()
+    kinds = len(places) // 2
+    part = edge // 2
+    for n, (i, j) in enumerate(places):
+        rows = pl.ds(n // kinds * part * kinds + n % kinds, part, kinds)
+        mix_ref[pl.ds(n * edge + core, part, 2), :] = own_ref[rows, :]
+        mix_ref[pl.ds(n * edge + 1 - core, part, 2), :] = twin_ref[rows, :]
         work_ref[i * edge : (i + 1) * edge, j * edge : (j + 1) * edge] = mix_ref[n * edge : (n + 1) * edge, :]
-    for i in range(1, count):
-        work_ref[i * edge : (i + 1) * edge, : i * edge] = jnp.zeros((edge, i * edge), F32)
+    everywhere = lax.broadcasted_iota(jnp.int32, (edge, size), 1)
 
     def stage(k, carry):
         base = pl.multiple_of(k * edge, edge)
-        rows = [work_ref[pl.ds(base + SUB * h, SUB), pl.ds(base, edge)] for h in range(edge // SUB)]
-        w = jnp.concatenate(eliminate(rows, edge), axis=0)
+        row_ref[...] = work_ref[pl.ds(base, edge), :]
+        for n in range(1, count):
+
+            @pl.when(k == n)
+            def _():
+                at = slice(n * edge, (n + 1) * edge)
+                above = slice(0, n * edge)
+                beyond = slice(n * edge, size)
+
+                def product(ref, lanes):
+                    return lax.dot_general(
+                        work_ref[above, at], ref[above, lanes], (((0,), (0,)), ((), ())),
+                        precision=hi, preferred_element_type=F32)
+
+                row_ref[:, beyond] = row_ref[:, beyond] - product(work_ref, beyond)
+                row_ref[:, above] = -product(inv_ref, above)
+
+        rows = [row_ref[SUB * h : SUB * (h + 1), pl.ds(base, edge)] for h in range(edge // SUB)]
+        w = jnp.concatenate(eliminate(rows, edge, zero_ref[...]), axis=0)
         r2 = lax.broadcasted_iota(jnp.int32, (edge, edge), 0)
         c2 = lax.broadcasted_iota(jnp.int32, (edge, edge), 1)
         inv = jnp.where(r2 >= c2, w, 0.0)
-        row_ref[...] = jnp.dot(inv, work_ref[pl.ds(base, edge), :], precision=hi, preferred_element_type=F32)
-        row_ref[:, pl.ds(base, edge)] = inv
-        work_ref[pl.ds(base, edge), :] = row_ref[...]
-
-        def below(i, carry):
-            at = pl.multiple_of(i * edge, edge)
-            work_ref[pl.ds(at, edge), pl.ds(base, edge)] = jnp.zeros((edge, edge), F32)
-            work_ref[pl.ds(at, edge), :] -= lax.dot_general(
-                row_ref[:, pl.ds(at, edge)], row_ref[...], (((0,), (0,)), ((), ())),
-                precision=hi, preferred_element_type=F32)
-            return carry
-
-        return lax.fori_loop(k + 1, count, below, carry)
+        done = jnp.dot(inv, row_ref[...], precision=hi, preferred_element_type=F32)
+        work_ref[pl.ds(base, edge), :] = done
+        inv_ref[pl.ds(base, edge), :] = jnp.where(everywhere < base, done, 0.0)
+        inv_ref[pl.ds(base, edge), pl.ds(base, edge)] = inv
+        return carry
 
     lax.fori_loop(0, count, stage, 0)
-    for i in range(count - 1):
-        work_ref[i * edge : (i + 1) * edge, (i + 1) * edge :] = jnp.zeros((edge, size - (i + 1) * edge), F32)
     width = mine_ref.shape[1]
-    first = ids_ref[0] == 0
+    first = side == 0
     left = jnp.where(first, mine_ref[...], other_ref[...])
     right = jnp.where(first, other_ref[...], mine_ref[...])
-    rest = work_ref[pl.ds(pl.multiple_of(ids_ref[0] * width, width), width), :]
+    rest = inv_ref[pl.ds(pl.multiple_of(side * width, width), width), :]
     total = jnp.zeros(out_ref.shape, F32)
     for _ in range(3):
         step = rest.astype(jnp.bfloat16)
@@ -134,20 +150,22 @@
     out_ref[...] = total
 
 
-def basis(ids, own, twin, mine, other):
-    edge, size = 2 * own.shape[0], 2 * mine.shape[1]
+def basis(side, core, own, twin, mine, other):
+    edge, size = own.shape[1], 2 * mine.shape[1]
+    scratch = [(size, size), (size, size), (edge, size), (2 * own.shape[0], edge), (SUB, edge)]
     return pl.pallas_call(
         basis_body,
         out_shape=jax.ShapeDtypeStruct(mine.shape, F32),
-        in_specs=[pl.BlockSpec(memory_space=pltpu.SMEM)] + [pl.BlockSpec(memory_space=pltpu.VMEM)] * 4,
+        in_specs=[pl.BlockSpec(memory_space=pltpu.SMEM)] * 2 + [pl.BlockSpec(memory_space=pltpu.VMEM)] * 4,
         out_specs=pl.BlockSpec(memory_space=pltpu.VMEM),
-        scratch_shapes=[pltpu.VMEM((size, size), F32), pltpu.VMEM((edge, size), F32), pltpu.VMEM((own.size // edge * 2, edge), F32)],
-    )(ids, own, twin, mine, other)
-
-
-def gram_body(side_ref, mine_ref, other_ref, packed_ref):
-    edge = packed_ref.shape[0]
+        scratch_shapes=[pltpu.VMEM(shape, F32) for shape in scratch],
+    )(side, core, own, twin, mine, other)
+
+
+def gram_body(side_ref, core_ref, mine_ref, other_ref, keep_ref, send_ref, mix_ref):
+    edge = mix_ref.shape[1]
     first = side_ref[0] == 0
+    core = core_ref[0]
     mine = mine_ref[...]
     other = other_ref[...]
     left = jnp.where(first, mine, other)
@@ -159,17 +177,23 @@
     own = product(mine, mine)
     cross = product(left, right)
     pieces = (own[:edge, :edge], own[:edge, edge:], own[edge:, edge:], cross[:edge], cross[edge:])
+    kinds, part = len(pieces), edge // 2
     for n, piece in enumerate(pieces):
-        packed_ref[:, n * edge : (n + 1) * edge] = piece
-
-
-def pair_gram(side, mine, other, edge):
+        mix_ref[n * edge : (n + 1) * edge, :] = piece
+        keep_ref[pl.ds(n, part, kinds), :] = mix_ref[pl.ds(n * edge + core, part, 2), :]
+        send_ref[pl.ds(n, part, kinds), :] = mix_ref[pl.ds(n * edge + 1 - core, part, 2), :]
+
+
+def pair_gram(side, core, mine, other, edge):
+    kinds = len(block_places()) // 2
+    piece = jax.ShapeDtypeStruct((edge // 2 * kinds, edge), F32)
     return pl.pallas_call(
         gram_body,
-        out_shape=jax.ShapeDtypeStruct((edge, 5 * edge), F32),
-        in_specs=[pl.BlockSpec(memory_space=pltpu.SMEM)] + [pl.BlockSpec(memory_space=pltpu.VMEM)] * 2,
-        out_specs=pl.BlockSpec(memory_space=pltpu.VMEM),
-    )(side, mine, other)
+        out_shape=(piece, piece),
+        in_specs=[pl.BlockSpec(memory_space=pltpu.SMEM)] * 2 + [pl.BlockSpec(memory_space=pltpu.VMEM)] * 2,
+        out_specs=(pl.BlockSpec(memory_space=pltpu.VMEM),) * 2,
+        scratch_shapes=[pltpu.VMEM((kinds * edge, edge), F32)],
+    )(side, core, mine, other)
 
 
 def local(tiles, tile_rows, tile_cols, tile_count, sketch, variant_scale):
@@ -217,23 +241,24 @@
         ).astype(bf16)
 
     scaled = (kept_scale * kept_rows.astype(f32)).astype(bf16)
-    range_rows = lax.optimization_barrier(forward(scaled))
+    squared = kept_scale * kept_scale
+    range_rows, squared, gather_back = lax.optimization_barrier((forward(scaled), squared, picks))
     terms = jnp.dot(wide, range_rows, preferred_element_type=f32).astype(bf16)
     arrived = spread(terms.reshape(owners, slots, width), GROUPS).reshape(owners * slots, width)
-    back = lax.dot_general(picks, arrived, (((0,), (0,)), ((), ())), preferred_element_type=f32)
-    weighted = ((kept_scale * kept_scale) * back).astype(bf16)
+    back = lax.dot_general(gather_back, arrived, (((0,), (0,)), ((), ())), preferred_element_type=f32)
+    weighted = (squared * back).astype(bf16)
     power_rows = forward(lax.optimization_barrier(weighted))
 
-    side = lax.axis_index("col")
+    side = lax.axis_index("col").reshape(1)
+    core = lax.axis_index("core").reshape(1)
     other = lax.ppermute(power_rows, "col", [(0, 1), (1, 0)])
-    packed_gram = pair_gram(side.reshape(1), power_rows, other, edge)
+    keep, send = pair_gram(side, core, power_rows, other, edge)
     total_rows = power_rows.shape[0] * owners
-    share = spread(packed_gram.reshape(owners, 1, -1), GROUPS).sum(0) / total_rows
-    own = spread(jnp.broadcast_to(share, (owners,) + share.shape), CHIPS + ("col",))
+    chip = keep + lax.ppermute(send, "core", [(0, 1), (1, 0)])
+    share = spread(chip.reshape(owners // 2, 1, -1), CHIPS).sum(0) / total_rows
+    own = spread(jnp.broadcast_to(share, (owners,) + share.shape), ("col",) + CHIPS)
     twin = lax.ppermute(own, "core", [(0, 1), (1, 0)])
-    ids = jnp.stack([side, lax.axis_index("core")])
-    half = (owners // 2, -1)
-    return basis(ids, own.reshape(half), twin.reshape(half), power_rows, other)
+    return basis(side, core, own.reshape(-1, edge), twin.reshape(-1, edge), power_rows, other)
 
 
 def solution(mesh):

time: 279 us -> 266 us (0.953)
  blocking collectives: 120 us -> 163 us
  waiting for transfers between devices: 81.5 us -> 43.1 us
  starting transfers between devices: 20.3 us -> 13.7 us
  Pallas kernels: 27.1 us -> 21.3 us
  local copies, waits for them, and re-layouts: 7.5 us -> 4.56 us
    all_to_all x4 -> x5, blocking collectives: 120 us -> 163 us  [spread(): return lax.all_to_all(rows, axes, split_axis=0, concat_axis=0, tiled=True)]
    all_to_all x2 -> x1, waiting for transfers between devices: 75.1 us -> 34.2 us  [spread(): return lax.all_to_all(rows, axes, split_axis=0, concat_axis=0, tiled=True)]
    all_to_all x2 -> x1, starting transfers between devices: 14.2 us -> 6.53 us  [spread(): return lax.all_to_all(rows, axes, split_axis=0, concat_axis=0, tiled=True)]
    pallas_call x1, Pallas kernels: 25 us -> 19.2 us  [basis(): pl.pallas_call(basis_body, out_shape=jax.ShapeDtypeStruct(mine.shape, F32...]
    reshape x4 -> x0, local copies, waits for them, and re-layouts: 3.04 us -> none  [the longest x2 1.63 us: local(): return basis(ids, own.reshape(half), twin.reshape(half), power_rows, other)]
  transfers between devices with their start and end apart: 4 -> 4, of which waited for: 3 -> 4; matrix products, arithmetic and copies ran while one was open for 2% -> 2% of each run, Pallas kernels for 0% -> 0%
where the time goes in v2:
time: 266 us; the launch traced here: 265 us
  blocking collectives  163 us (61%)
  waiting for transfers between devices  43.1 us (16%)
  Pallas kernels  21.3 us (8%)
  starting transfers between devices  13.7 us (5%)
  matrix products  11 us (4%)
  other arithmetic  7.69 us (3%)
  local copies, waits for them, and re-layouts  4.56 us (2%)
    all_to_all x5, blocking collectives, spread(): return lax.all_to_all(rows, axes, split_axis=0, concat_axis=0, tiled=True)  163 us
    all_to_all x1, waiting for transfers between devices, spread(): return lax.all_to_all(rows, axes, split_axis=0, concat_axis=0, tiled=True)  34.2 us
    pallas_call x1, Pallas kernels, basis(): pl.pallas_call(basis_body, out_shape=jax.ShapeDtypeStruct(mine.shape, F32...  19.2 us
    all_to_all x1, starting transfers between devices, spread(): return lax.all_to_all(rows, axes, split_axis=0, concat_axis=0, tiled=True)  6.53 us
    ppermute x1, waiting for transfers between devices, local(): other = lax.ppermute(power_rows, 'col', [(0, 1), (1, 0)])  6.34 us
  transfers between devices with their start and end apart: 4, of which 4 were waited for; matrix products, arithmetic and copies ran while one was open for 2% of the time, Pallas kernels for 0%

profile of v2, /device:TPU:1, one launch (start us, length us, event | category | flops | bytes accessed | tf_op | source)
XLA Modules:
  0.0 265.4 jit_solution(5223953107405470174)
XLA Ops:
  0.7 1.1 copy.19
  1.8 0.7 fusion.25
  2.5 0.8 pad_maximum_fusion.1
  3.3 0.7 copy.20
  4.0 30.3 %all_to_all.30 = bf16[128,2,640]{2,1,0:T(2,128)(2,1)S(1)} all-to-all(bf16[128,2,640]{2,1,0:T(2,128)(2,1)S(1)} %copy.20), channel_id=1, replica_groups=mesh['z'=8,'y'=2,'x'=4,'core'=2,'col'=2] {'z','y','x','core'}, dimensions={0} | all-to-all | bytes 655360 | tf_op jit(solution)/shard_map/all_to_all | solution.py:15
  34.9 0.4 reshape.134
  35.3 2.6 fusion.3
  37.9 6.5 %all-to-all-start.1 = ((bf16[128,24,256]{2,1,0:T(8,128)(2,1)}), bf16[128,24,256]{2,1,0:T(8,128)(2,1)}, u32[]{:S(2)}, u32[]{:S(2)}) async-start(bf16[128,24,256]{2,1,0:T(8,128)(2,1)} %bitcast.10), calls=%async_computation.1 | async-start | bytes 3145728 | tf_op jit(solution)/shard_map/all_to_all | solution.py:15
  44.5 0.4 copy.18
  45.0 3.3 %broadcast_multiply_fusion = bf16[128,24,4,128]{3,2,1,0:T(4,128)(2,1)} fusion(bf16[24,4]{1,0:T(8,128)(2,1)S(1)} %fusion.24, bf16[128,24,128]{2,1,0:T(8,128)(2,1)S(1)} %copy.18), kind=kLoop, calls=%fused_computation.17 | loop fusion | flops 1572864 | bytes 3932352 | tf_op jit(solution)/shard_map/mul | solution.py:233
  48.4 1.4 fusion.1
  49.8 34.2 %all-to-all-done.1 = bf16[128,24,256]{2,1,0:T(8,128)(2,1)} async-done(((bf16[128,24,256]{2,1,0:T(8,128)(2,1)}), bf16[128,24,256]{2,1,0:T(8,128)(2,1)}, u32[]{:S(2)}, u32[]{:S(2)}) %all-to-all-start.1) | async-done | bytes 1572896 | tf_op jit(solution)/shard_map/all_to_all | solution.py:15
  84.0 3.5 %fusion.16 = bf16[512,256]{1,0:T(8,128)(2,1)S(1)} fusion(bf16[3072,256]{1,0:T(8,128)(2,1)} %bitcast.11, bf16[384,8,4,128]{3,2,1,0:T(4,128)(2,1)} %bitcast.47), kind=kOutput, calls=%fused_computation.20 | convolution fusion | flops 805437440 | bytes 4980736 | tf_op jit(solution)/shard_map/dot_general | solution.py:239
  87.5 1.0 convolution_convert_fusion
  88.5 47.2 %all_to_all.31 = bf16[128,24,256]{2,1,0:T(8,128)(2,1)S(1)} all-to-all(bf16[128,24,256]{2,1,0:T(8,128)(2,1)S(1)} %bitcast.52), channel_id=1, replica_groups=mesh['z'=8,'y'=2,'x'=4,'core'=2,'col'=2] {'z','y','x','core'}, dimensions={0} | all-to-all | bytes 3145728 | tf_op jit(solution)/shard_map/all_to_all | solution.py:15
  135.8 1.0 fusion.15
  136.8 1.7 fusion.4
  138.5 47.0 %all_to_all.32 = bf16[128,24,256]{2,1,0:T(8,128)(2,1)S(1)} all-to-all(bf16[128,24,256]{2,1,0:T(8,128)(2,1)S(1)} %bitcast.50), channel_id=1, replica_groups=mesh['z'=8,'y'=2,'x'=4,'core'=2,'col'=2] {'z','y','x','core'}, dimensions={0} | all-to-all | bytes 3145728 | tf_op jit(solution)/shard_map/all_to_all | solution.py:15
  185.5 1.1 fusion.19.mine_ref
  186.7 2.7 %collective-permute-start = (bf16[512,256]{1,0:T(8,128)(2,1)S(1)}, bf16[512,256]{1,0:T(8,128)(2,1)S(1)}, u32[]{:S(2)}, u32[]{:S(2)}) collective-permute-start(bf16[512,256]{1,0:T(8,128)(2,1)S(1)} %fusion.19.mine_ref), channel_id=1, source_target_pairs={{0,1},{1,0},{2,3},{3,2},{4,5},{5,4},{6,7},{7,6},{8,9},{9,8},{10,11... | collective-permute-start | bytes 786440 | tf_op jit(solution)/shard_map/ppermute | solution.py:254
  189.4 6.3 %collective-permute-done.other_ref = bf16[512,256]{1,0:T(8,128)(2,1)S(1)} collective-permute-done((bf16[512,256]{1,0:T(8,128)(2,1)S(1)}, bf16[512,256]{1,0:T(8,128)(2,1)S(1)}, u32[]{:S(2)}, u32[]{:S(2)}) %collective-permute-start) | collective-permute-done | bytes 262176 | tf_op jit(solution)/shard_map/ppermute | solution.py:254
  195.7 0.7 copy-done.3
  196.4 2.1 shard_map.64
  198.5 1.3 collective-permute-start.1
  199.8 1.2 collective-permute-done.1
  201.0 0.9 add.17
  202.0 15.6 %all_to_all.33 = f32[64,1,640]{2,1,0:T(1,128)S(1)} all-to-all(f32[64,1,640]{2,1,0:T(1,128)S(1)} %bitcast.58), channel_id=1, replica_groups=mesh['z'=8,'y'=2,'x'=4,'core'=2,'col'=2] {'z','y','x'}, dimensions={0} | all-to-all | bytes 327680 | tf_op jit(solution)/shard_map/all_to_all | solution.py:15
  217.8 23.1 %all_to_all.34 = f32[128,1,640]{2,1,0:T(1,128)S(1)} all-to-all(f32[128,1,640]{2,1,0:T(1,128)S(1)} %broadcast_in_dim.7), channel_id=1, replica_groups=mesh['z'=8,'y'=2,'x'=4,'core'=2,'col'=2] {'col','z','y','x'}, dimensions={0} | all-to-all | bytes 655360 | tf_op jit(solution)/shard_map/all_to_all | solution.py:15
  240.9 3.3 %collective-permute-start.2 = (f32[128,1,640]{2,1,0:T(1,128)S(1)}, f32[128,1,640]{2,1,0:T(1,128)S(1)}, u32[]{:S(2)}, u32[]{:S(2)}) collective-permute-start(f32[128,1,640]{2,1,0:T(1,128)S(1)} %all_to_all.34), channel_id=1, source_target_pairs={{0,2},{2,0},{1,3},{3,1},{4,6},{6,4},{5,7},{7,5},{8,10},{10,8},{9,1... | collective-permute-start | bytes 983048 | tf_op jit(solution)/shard_map/ppermute | solution.py:260
  244.2 1.3 collective-permute-done.2
  245.4 0.7 copy-done.5
  246.2 19.2 %shard_map.65 = f32[512,256]{1,0:T(8,128)} custom-call(s32[1]{0:T(128)} %bitcast.side_ref, s32[1]{0:T(128)} %bitcast.1.core_ref, f32[640,128]{1,0:T(8,128)} %bitcast.53, f32[640,128]{1,0:T(8,128)} %bitcast.60, bf16[512,256]{1,0:T(8,128)(2,1)} %copy-done.2, bf16[512,256]{1,0:T(8,128)(2,1)} %copy-done.3), custom_call_target="tpu_custom_call" | custom-call | tf_op jit(solution)/shard_map/pallas_call | solution.py:156
  (27 shorter events, 1.2 us)
Async XLA Ops:
  37.9 6.5 %copy-start.4 = (bf16[24,128,128]{2,1,0:T(8,128)(2,1)S(1)}, bf16[24,128,128]{2,1,0:T(8,128)(2,1)}, u32[]{:S(2)}) copy-start(bf16[24,128,128]{2,1,0:T(8,128)(2,1)} %param.6) | copy-start | bytes 2359300
  37.9 7.0 %copy-start.6 = (s32[24]{0:T(128)S(1)}, s32[24]{0:T(128)}, u32[]{:S(2)}) copy-start(s32[24]{0:T(128)} %param.7) | copy-start | bytes 292
  37.9 46.1 %all-to-all-start.1 = ((bf16[128,24,256]{2,1,0:T(8,128)(2,1)}), bf16[128,24,256]{2,1,0:T(8,128)(2,1)}, u32[]{:S(2)}, u32[]{:S(2)}) async-start(bf16[128,24,256]{2,1,0:T(8,128)(2,1)} %bitcast.10), calls=%async_computation.1 | async-start | bytes 3145728 | tf_op jit(solution)/shard_map/all_to_all | solution.py:15
  84.0 3.5 %copy-start = (bf16[128,24,4,128]{3,2,1,0:T(4,128)(2,1)S(1)}, bf16[128,24,4,128]{3,2,1,0:T(4,128)(2,1)}, u32[]{:S(2)}) copy-start(bf16[128,24,4,128]{3,2,1,0:T(4,128)(2,1)} %broadcast_multiply_fusion) | copy-start | bytes 9437188
  186.6 9.1 %copy-start.2 = (bf16[512,256]{1,0:T(8,128)(2,1)}, bf16[512,256]{1,0:T(8,128)(2,1)S(1)}, u32[]{:S(2)}) copy-start(bf16[512,256]{1,0:T(8,128)(2,1)S(1)} %fusion.19.mine_ref) | copy-start | bytes 786436
  186.7 9.1 %collective-permute-start = (bf16[512,256]{1,0:T(8,128)(2,1)S(1)}, bf16[512,256]{1,0:T(8,128)(2,1)S(1)}, u32[]{:S(2)}, u32[]{:S(2)}) collective-permute-start(bf16[512,256]{1,0:T(8,128)(2,1)S(1)} %fusion.19.mine_ref), channel_id=1, source_target_pairs={{0,1},{1,0},{2,3},{3,2},{4,5},{5,4},{6,7},{7,6},{8,9},{9,8},{10,11... | collective-permute-start | bytes 786440 | tf_op jit(solution)/shard_map/ppermute | solution.py:254
  195.7 0.7 copy-start.3
  198.5 2.5 collective-permute-start.1
  240.9 4.5 %copy-start.1 = (f32[128,1,640]{2,1,0:T(1,128)}, f32[128,1,640]{2,1,0:T(1,128)S(1)}, u32[]{:S(2)}) copy-start(f32[128,1,640]{2,1,0:T(1,128)S(1)} %all_to_all.34) | copy-start | bytes 983044
  240.9 4.5 %collective-permute-start.2 = (f32[128,1,640]{2,1,0:T(1,128)S(1)}, f32[128,1,640]{2,1,0:T(1,128)S(1)}, u32[]{:S(2)}, u32[]{:S(2)}) collective-permute-start(f32[128,1,640]{2,1,0:T(1,128)S(1)} %all_to_all.34), channel_id=1, source_target_pairs={{0,2},{2,0},{1,3},{3,1},{4,6},{6,4},{5,7},{7,5},{8,10},{10,8},{9,1... | collective-permute-start | bytes 983048 | tf_op jit(solution)/shard_map/ppermute | solution.py:260
  245.4 0.7 copy-start.5

commit v3 on v2

--- a/solution.py
+++ b/solution.py
@@ -153,6 +153,7 @@
 def basis(side, core, own, twin, mine, other):
     edge, size = own.shape[1], 2 * mine.shape[1]
     scratch = [(size, size), (size, size), (edge, size), (2 * own.shape[0], edge), (SUB, edge)]
+    own, twin, mine, other = (pltpu.with_memory_space_constraint(v, pltpu.VMEM) for v in (own, twin, mine, other))
     return pl.pallas_call(
         basis_body,
         out_shape=jax.ShapeDtypeStruct(mine.shape, F32),
@@ -186,7 +187,8 @@
 
 def pair_gram(side, core, mine, other, edge):
     kinds = len(block_places()) // 2
-    piece = jax.ShapeDtypeStruct((edge // 2 * kinds, edge), F32)
+    piece = pltpu.VMEM((edge // 2 * kinds, edge), F32)
+    mine, other = (pltpu.with_memory_space_constraint(v, pltpu.VMEM) for v in (mine, other))
     return pl.pallas_call(
         gram_body,
         out_shape=(piece, piece),
@@ -216,7 +218,12 @@
     packed = jnp.concatenate(
         [own_rows.reshape(edge, 2, -1), notes.reshape(edge, 2, -1)], axis=2
     )
-    kept = spread(packed, GROUPS)
+    row_ids = jnp.arange(RB_DEV, dtype=jnp.int32)
+    row_mask = (tile_rows[:, None] == row_ids).astype(bf16)
+    turned = jnp.transpose(tiles, (2, 0, 1))
+    wide = turned[:, :, None, :] * row_mask[None, :, :, None]
+    wide = wide.reshape(edge * slots, RB_DEV * edge)
+    kept, wide = lax.optimization_barrier((spread(packed, GROUPS), wide))
     row_part = own_blocks // 2 * width
     kept_rows = kept[:, :, :row_part].reshape(blocks, width)
     kept_notes = kept[:, :, row_part:].reshape(owners, width).astype(f32)
@@ -226,12 +233,8 @@
     all_cols = (all_runs * own_blocks + all_members).astype(jnp.int32)
     block_ids = jnp.arange(blocks, dtype=jnp.int32)
     picks = (all_cols[:, :, None] == block_ids).astype(bf16).reshape(owners * slots, blocks)
-
-    row_ids = jnp.arange(RB_DEV, dtype=jnp.int32)
-    row_mask = (tile_rows[:, None] == row_ids).astype(bf16)
-    turned = jnp.transpose(tiles, (2, 0, 1))
-    wide = turned[:, :, None, :] * row_mask[None, :, :, None]
-    wide = wide.reshape(edge * slots, RB_DEV * edge)
+    squared = kept_scale * kept_scale
+    picks, squared = lax.optimization_barrier((picks, squared))
 
     def forward(kept_operand):
         sent = jnp.dot(picks, kept_operand, preferred_element_type=f32).astype(bf16)
@@ -241,11 +244,10 @@
         ).astype(bf16)
 
     scaled = (kept_scale * kept_rows.astype(f32)).astype(bf16)
-    squared = kept_scale * kept_scale
-    range_rows, squared, gather_back = lax.optimization_barrier((forward(scaled), squared, picks))
+    range_rows = lax.optimization_barrier(forward(scaled))
     terms = jnp.dot(wide, range_rows, preferred_element_type=f32).astype(bf16)
     arrived = spread(terms.reshape(owners, slots, width), GROUPS).reshape(owners * slots, width)
-    back = lax.dot_general(gather_back, arrived, (((0,), (0,)), ((), ())), preferred_element_type=f32)
+    back = lax.dot_general(picks, arrived, (((0,), (0,)), ((), ())), preferred_element_type=f32)
     weighted = (squared * back).astype(bf16)
     power_rows = forward(lax.optimization_barrier(weighted))
 

time: 266 us -> 261 us (0.981)
  waiting for transfers between devices: 43.1 us -> 20 us
  blocking collectives: 163 us -> 178 us
  starting transfers between devices: 13.7 us -> 22.1 us
  matrix products: 11 us -> 7.15 us
  local copies, waits for them, and re-layouts: 4.56 us -> 7.67 us
  Pallas kernels: 21.3 us -> 18.3 us
    all_to_all x1, waiting for transfers between devices: 34.2 us -> 11.3 us  [spread(): return lax.all_to_all(rows, axes, split_axis=0, concat_axis=0, tiled=True)]
    all_to_all x5, blocking collectives: 163 us -> 178 us  [spread(): return lax.all_to_all(rows, axes, split_axis=0, concat_axis=0, tiled=True)]
    all_to_all x1, starting transfers between devices: 6.53 us -> 14.8 us  [spread(): return lax.all_to_all(rows, axes, split_axis=0, concat_axis=0, tiled=True)]
where the time goes in v3:
time: 261 us; the launch traced here: 260 us
  blocking collectives  178 us (68%)
  starting transfers between devices  22.1 us (8%)
  waiting for transfers between devices  20 us (8%)
  Pallas kernels  18.3 us (7%)
  local copies, waits for them, and re-layouts  7.67 us (3%)
  matrix products  7.15 us (3%)
  other arithmetic  5.94 us (2%)
    all_to_all x5, blocking collectives, spread(): return lax.all_to_all(rows, axes, split_axis=0, concat_axis=0, tiled=True)  178 us
    pallas_call x1, Pallas kernels, basis(): pl.pallas_call(basis_body, out_shape=jax.ShapeDtypeStruct(mine.shape, F32...  18 us
    all_to_all x1, starting transfers between devices, spread(): return lax.all_to_all(rows, axes, split_axis=0, concat_axis=0, tiled=True)  14.8 us
    all_to_all x1, waiting for transfers between devices, spread(): return lax.all_to_all(rows, axes, split_axis=0, concat_axis=0, tiled=True)  11.3 us
    ppermute x1, waiting for transfers between devices, local(): other = lax.ppermute(power_rows, 'col', [(0, 1), (1, 0)])  6.35 us
  transfers between devices with their start and end apart: 4, of which 4 were waited for; matrix products, arithmetic and copies ran while one was open for 2% of the time, Pallas kernels for 0%

profile of v3, /device:TPU:1, one launch (start us, length us, event | category | flops | bytes accessed | tf_op | source)
XLA Modules:
  0.0 260.1 jit_solution(66769866057238253)
XLA Ops:
  0.7 1.1 copy.18
  1.9 0.7 fusion.5
  2.6 0.8 pad_maximum_fusion.1
  3.4 1.2 copy.19
  4.6 14.8 %all-to-all-start = ((bf16[128,2,640]{2,1,0:T(2,128)(2,1)}), bf16[128,2,640]{2,1,0:T(2,128)(2,1)S(1)}, u32[]{:S(2)}, u32[]{:S(2)}) async-start(bf16[128,2,640]{2,1,0:T(2,128)(2,1)} %copy.19), calls=%async_computation | async-start | bytes 655360 | tf_op jit(solution)/shard_map/all_to_all | solution.py:15
  19.4 0.4 copy.20
  19.9 1.7 broadcast_multiply_fusion
  21.6 2.2 copy.26
  23.7 11.3 %all-to-all-done = bf16[128,2,640]{2,1,0:T(2,128)(2,1)S(1)} async-done(((bf16[128,2,640]{2,1,0:T(2,128)(2,1)}), bf16[128,2,640]{2,1,0:T(2,128)(2,1)S(1)}, u32[]{:S(2)}, u32[]{:S(2)}) %all-to-all-start) | async-done | bytes 327712 | tf_op jit(solution)/shard_map/all_to_all | solution.py:15
  35.2 1.0 slice_convert_fusion
  36.4 1.4 fusion
  37.9 2.3 reshape.119
  40.2 2.1 convolution_convert_fusion.2
  42.3 45.1 %all_to_all.30 = bf16[128,24,256]{2,1,0:T(8,128)(2,1)S(1)} all-to-all(bf16[128,24,256]{2,1,0:T(8,128)(2,1)S(1)} %bitcast.49), channel_id=1, replica_groups=mesh['z'=8,'y'=2,'x'=4,'core'=2,'col'=2] {'z','y','x','core'}, dimensions={0} | all-to-all | bytes 3145728 | tf_op jit(solution)/shard_map/all_to_all | solution.py:15
  87.5 1.0 convolution_convert_fusion.4
  88.5 1.0 convolution_convert_fusion.1
  89.5 47.2 %all_to_all.31 = bf16[128,24,256]{2,1,0:T(8,128)(2,1)S(1)} all-to-all(bf16[128,24,256]{2,1,0:T(8,128)(2,1)S(1)} %bitcast.54), channel_id=1, replica_groups=mesh['z'=8,'y'=2,'x'=4,'core'=2,'col'=2] {'z','y','x','core'}, dimensions={0} | all-to-all | bytes 3145728 | tf_op jit(solution)/shard_map/all_to_all | solution.py:15
  136.7 1.0 fusion.1
  137.7 1.0 convolution_convert_fusion
  138.7 47.0 %all_to_all.32 = bf16[128,24,256]{2,1,0:T(8,128)(2,1)S(1)} all-to-all(bf16[128,24,256]{2,1,0:T(8,128)(2,1)S(1)} %bitcast.53), channel_id=1, replica_groups=mesh['z'=8,'y'=2,'x'=4,'core'=2,'col'=2] {'z','y','x','core'}, dimensions={0} | all-to-all | bytes 3145728 | tf_op jit(solution)/shard_map/all_to_all | solution.py:15
  185.8 1.0 convolution_convert_fusion.3.mine_ref
  186.8 2.7 %collective-permute-start = (bf16[512,256]{1,0:T(8,128)(2,1)S(1)}, bf16[512,256]{1,0:T(8,128)(2,1)S(1)}, u32[]{:S(2)}, u32[]{:S(2)}) collective-permute-start(bf16[512,256]{1,0:T(8,128)(2,1)S(1)} %convolution_convert_fusion.3.mine_ref), channel_id=1, source_target_pairs={{0,1},{1,0},{2,3},{3,2},{4,5},{5,4},{6,7},{7,6},{8,9},{9,8},{10,11... | collective-permute-start | bytes 786440 | tf_op jit(solution)/shard_map/ppermute | solution.py:256
  189.5 6.4 %collective-permute-done.other_ref = bf16[512,256]{1,0:T(8,128)(2,1)S(1)} collective-permute-done((bf16[512,256]{1,0:T(8,128)(2,1)S(1)}, bf16[512,256]{1,0:T(8,128)(2,1)S(1)}, u32[]{:S(2)}, u32[]{:S(2)}) %collective-permute-start) | collective-permute-done | bytes 262176 | tf_op jit(solution)/shard_map/ppermute | solution.py:256
  195.9 0.4 shard_map.64
  196.2 1.3 collective-permute-start.1
  197.6 1.0 collective-permute-done.1
  198.6 15.6 %all_to_all.33 = f32[64,1,640]{2,1,0:T(1,128)S(1)} all-to-all(f32[64,1,640]{2,1,0:T(1,128)S(1)} %bitcast.59), channel_id=1, replica_groups=mesh['z'=8,'y'=2,'x'=4,'core'=2,'col'=2] {'z','y','x'}, dimensions={0} | all-to-all | bytes 327680 | tf_op jit(solution)/shard_map/all_to_all | solution.py:15
  214.3 0.2 broadcast_in_dim.7
  214.5 23.1 %all_to_all.34 = f32[128,1,640]{2,1,0:T(1,128)S(1)} all-to-all(f32[128,1,640]{2,1,0:T(1,128)S(1)} %broadcast_in_dim.7), channel_id=1, replica_groups=mesh['z'=8,'y'=2,'x'=4,'core'=2,'col'=2] {'col','z','y','x'}, dimensions={0} | all-to-all | bytes 655360 | tf_op jit(solution)/shard_map/all_to_all | solution.py:15
  237.6 3.3 %collective-permute-start.2 = (f32[128,1,640]{2,1,0:T(1,128)S(1)}, f32[128,1,640]{2,1,0:T(1,128)S(1)}, u32[]{:S(2)}, u32[]{:S(2)}) collective-permute-start(f32[128,1,640]{2,1,0:T(1,128)S(1)} %all_to_all.34), channel_id=1, source_target_pairs={{0,2},{2,0},{1,3},{3,1},{4,6},{6,4},{5,7},{7,5},{8,10},{10,8},{9,1... | collective-permute-start | bytes 983048 | tf_op jit(solution)/shard_map/ppermute | solution.py:262
  240.8 1.3 collective-permute-done.2
  242.1 18.0 %shard_map.65 = f32[512,256]{1,0:T(8,128)} custom-call(s32[1]{0:T(128)} %bitcast.side_ref, s32[1]{0:T(128)} %bitcast.1.core_ref, f32[640,128]{1,0:T(8,128)S(1)} %bitcast.43, f32[640,128]{1,0:T(8,128)S(1)} %bitcast.44, bf16[512,256]{1,0:T(8,128)(2,1)S(1)} %convolution_convert_fusion.3.mine_ref, bf16[512,256]{1,0:T(8,128)(2,1)S(1)} %collective-permute-done.other_ref), custom_call_target="tpu_custom_call" | custom-call | tf_op jit(solution)/shard_map/pallas_call | solution.py:157
  (20 shorter events, 0.8 us)
Async XLA Ops:
  0.0 19.4 %copy-start.1 = (bf16[24,128,128]{2,1,0:T(8,128)(2,1)S(1)}, bf16[24,128,128]{2,1,0:T(8,128)(2,1)}, u32[]{:S(2)}) copy-start(bf16[24,128,128]{2,1,0:T(8,128)(2,1)} %param.6) | copy-start | bytes 2359300
  0.0 19.8 %copy-start.2 = (s32[24]{0:T(128)S(1)}, s32[24]{0:T(128)}, u32[]{:S(2)}) copy-start(s32[24]{0:T(128)} %param.7) | copy-start | bytes 292
  4.6 30.5 %all-to-all-start = ((bf16[128,2,640]{2,1,0:T(2,128)(2,1)}), bf16[128,2,640]{2,1,0:T(2,128)(2,1)S(1)}, u32[]{:S(2)}, u32[]{:S(2)}) async-start(bf16[128,2,640]{2,1,0:T(2,128)(2,1)} %copy.19), calls=%async_computation | async-start | bytes 655360 | tf_op jit(solution)/shard_map/all_to_all | solution.py:15
  42.3 45.2 %copy-start = (bf16[384,8,4,128]{3,1,2,0:T(8,128)(2,1)S(1)}, bf16[384,8,4,128]{3,1,2,0:T(8,128)(2,1)}, u32[]{:S(2)}) copy-start(bf16[384,8,4,128]{3,1,2,0:T(8,128)(2,1)} %copy.26) | copy-start | bytes 9437188
  186.8 9.1 %collective-permute-start = (bf16[512,256]{1,0:T(8,128)(2,1)S(1)}, bf16[512,256]{1,0:T(8,128)(2,1)S(1)}, u32[]{:S(2)}, u32[]{:S(2)}) collective-permute-start(bf16[512,256]{1,0:T(8,128)(2,1)S(1)} %convolution_convert_fusion.3.mine_ref), channel_id=1, source_target_pairs={{0,1},{1,0},{2,3},{3,2},{4,5},{5,4},{6,7},{7,6},{8,9},{9,8},{10,11... | collective-permute-start | bytes 786440 | tf_op jit(solution)/shard_map/ppermute | solution.py:256
  196.2 2.4 collective-permute-start.1
  237.6 4.5 %collective-permute-start.2 = (f32[128,1,640]{2,1,0:T(1,128)S(1)}, f32[128,1,640]{2,1,0:T(1,128)S(1)}, u32[]{:S(2)}, u32[]{:S(2)}) collective-permute-start(f32[128,1,640]{2,1,0:T(1,128)S(1)} %all_to_all.34), channel_id=1, source_target_pairs={{0,2},{2,0},{1,3},{3,1},{4,6},{6,4},{5,7},{7,5},{8,10},{10,8},{9,1... | collective-permute-start | bytes 983048 | tf_op jit(solution)/shard_map/ppermute | solution.py:262

commit v4 on v3

--- a/solution.py
+++ b/solution.py
@@ -207,7 +207,8 @@
     blocks = owners * own_blocks
     bf16, f32 = jnp.bfloat16, jnp.float32
 
-    own_rows = jnp.swapaxes(sketch.reshape(own_blocks, edge, width), 0, 1)
+    scaled = (variant_scale.astype(f32)[:, None] * sketch.astype(f32)).astype(bf16)
+    own_rows = jnp.swapaxes(scaled.reshape(own_blocks, edge, width), 0, 1)
     own_scales = variant_scale.reshape(own_blocks, edge).T
     live = jnp.arange(slots, dtype=jnp.int32) < tile_count[0]
     run = jnp.where(live, tile_cols // own_blocks, -1).astype(bf16)
@@ -223,7 +224,7 @@
     turned = jnp.transpose(tiles, (2, 0, 1))
     wide = turned[:, :, None, :] * row_mask[None, :, :, None]
     wide = wide.reshape(edge * slots, RB_DEV * edge)
-    kept, wide = lax.optimization_barrier((spread(packed, GROUPS), wide))
+    kept = spread(packed, GROUPS)
     row_part = own_blocks // 2 * width
     kept_rows = kept[:, :, :row_part].reshape(blocks, width)
     kept_notes = kept[:, :, row_part:].reshape(owners, width).astype(f32)
@@ -234,7 +235,7 @@
     block_ids = jnp.arange(blocks, dtype=jnp.int32)
     picks = (all_cols[:, :, None] == block_ids).astype(bf16).reshape(owners * slots, blocks)
     squared = kept_scale * kept_scale
-    picks, squared = lax.optimization_barrier((picks, squared))
+    picks, squared, wide = lax.optimization_barrier((picks, squared, wide))
 
     def forward(kept_operand):
         sent = jnp.dot(picks, kept_operand, preferred_element_type=f32).astype(bf16)
@@ -243,8 +244,7 @@
             wide, fetched, (((0,), (0,)), ((), ())), preferred_element_type=f32
         ).astype(bf16)
 
-    scaled = (kept_scale * kept_rows.astype(f32)).astype(bf16)
-    range_rows = lax.optimization_barrier(forward(scaled))
+    range_rows = lax.optimization_barrier(forward(kept_rows))
     terms = jnp.dot(wide, range_rows, preferred_element_type=f32).astype(bf16)
     arrived = spread(terms.reshape(owners, slots, width), GROUPS).reshape(owners * slots, width)
     back = lax.dot_general(picks, arrived, (((0,), (0,)), ((), ())), preferred_element_type=f32)

time: 261 us -> 260 us (level)
  transfers between devices with their start and end apart: 4 -> 4, of which waited for: 4 -> 4; matrix products, arithmetic and copies ran while one was open for 2% -> 1% of each run, Pallas kernels for 0% -> 0%
where the time goes in v4:
time: 260 us
  blocking collectives  178 us (68%)
  starting transfers between devices  22.1 us (8%)
  waiting for transfers between devices  21.6 us (8%)
  Pallas kernels  18.3 us (7%)
  other arithmetic  7.35 us (3%)
  matrix products  6 us (2%)
  local copies, waits for them, and re-layouts  5.56 us (2%)
    all_to_all x5, blocking collectives, spread(): return lax.all_to_all(rows, axes, split_axis=0, concat_axis=0, tiled=True)  178 us
    pallas_call x1, Pallas kernels, basis(): pl.pallas_call(basis_body, out_shape=jax.ShapeDtypeStruct(mine.shape, F32...  18 us
    all_to_all x1, starting transfers between devices, spread(): return lax.all_to_all(rows, axes, split_axis=0, concat_axis=0, tiled=True)  14.8 us
    all_to_all x1, waiting for transfers between devices, spread(): return lax.all_to_all(rows, axes, split_axis=0, concat_axis=0, tiled=True)  12.9 us
    ppermute x1, waiting for transfers between devices, local(): other = lax.ppermute(power_rows, 'col', [(0, 1), (1, 0)])  6.35 us
  transfers between devices with their start and end apart: 4, of which 4 were waited for; matrix products, arithmetic and copies ran while one was open for 1% of the time, Pallas kernels for 0%

profile of v4, /device:TPU:1, one launch (start us, length us, event | category | flops | bytes accessed | tf_op | source)
XLA Modules:
  0.0 259.9 jit_solution(718701093893416720)
XLA Ops:
  0.7 0.7 convert_element_type.55
  1.4 1.1 multiply_convert_fusion
  2.7 0.7 fusion.4
  3.4 0.8 pad_maximum_fusion.1
  4.2 1.2 copy.19
  5.4 14.8 %all-to-all-start = ((bf16[128,2,640]{2,1,0:T(2,128)(2,1)}), bf16[128,2,640]{2,1,0:T(2,128)(2,1)S(1)}, u32[]{:S(2)}, u32[]{:S(2)}) async-start(bf16[128,2,640]{2,1,0:T(2,128)(2,1)} %copy.19), calls=%async_computation | async-start | bytes 655360 | tf_op jit(solution)/shard_map/all_to_all | solution.py:15
  20.7 1.7 broadcast_multiply_fusion
  22.4 0.5 copy.26
  22.9 12.9 %all-to-all-done = bf16[128,2,640]{2,1,0:T(2,128)(2,1)S(1)} async-done(((bf16[128,2,640]{2,1,0:T(2,128)(2,1)}), bf16[128,2,640]{2,1,0:T(2,128)(2,1)S(1)}, u32[]{:S(2)}, u32[]{:S(2)}) %all-to-all-start) | async-done | bytes 327712 | tf_op jit(solution)/shard_map/all_to_all | solution.py:15
  36.1 0.6 slice_multiply_fusion
  36.7 0.9 slice.24
  37.6 1.1 reshape.109
  38.7 0.9 mul.60
  39.7 1.4 fusion
  41.1 1.0 convolution_convert_fusion.2
  42.1 44.9 %all_to_all.30 = bf16[128,24,256]{2,1,0:T(8,128)(2,1)S(1)} all-to-all(bf16[128,24,256]{2,1,0:T(8,128)(2,1)S(1)} %bitcast.54), channel_id=1, replica_groups=mesh['z'=8,'y'=2,'x'=4,'core'=2,'col'=2] {'z','y','x','core'}, dimensions={0} | all-to-all | bytes 3145728 | tf_op jit(solution)/shard_map/all_to_all | solution.py:15
  87.0 1.0 convolution_convert_fusion.4
  88.0 1.0 convolution_convert_fusion.1
  89.0 47.2 %all_to_all.31 = bf16[128,24,256]{2,1,0:T(8,128)(2,1)S(1)} all-to-all(bf16[128,24,256]{2,1,0:T(8,128)(2,1)S(1)} %bitcast.55), channel_id=1, replica_groups=mesh['z'=8,'y'=2,'x'=4,'core'=2,'col'=2] {'z','y','x','core'}, dimensions={0} | all-to-all | bytes 3145728 | tf_op jit(solution)/shard_map/all_to_all | solution.py:15
  136.2 1.0 fusion.1
  137.3 1.0 convolution_convert_fusion
  138.3 47.3 %all_to_all.32 = bf16[128,24,256]{2,1,0:T(8,128)(2,1)S(1)} all-to-all(bf16[128,24,256]{2,1,0:T(8,128)(2,1)S(1)} %bitcast.53), channel_id=1, replica_groups=mesh['z'=8,'y'=2,'x'=4,'core'=2,'col'=2] {'z','y','x','core'}, dimensions={0} | all-to-all | bytes 3145728 | tf_op jit(solution)/shard_map/all_to_all | solution.py:15
  185.6 1.0 convolution_convert_fusion.3.mine_ref
  186.6 2.7 %collective-permute-start = (bf16[512,256]{1,0:T(8,128)(2,1)S(1)}, bf16[512,256]{1,0:T(8,128)(2,1)S(1)}, u32[]{:S(2)}, u32[]{:S(2)}) collective-permute-start(bf16[512,256]{1,0:T(8,128)(2,1)S(1)} %convolution_convert_fusion.3.mine_ref), channel_id=1, source_target_pairs={{0,1},{1,0},{2,3},{3,2},{4,5},{5,4},{6,7},{7,6},{8,9},{9,8},{10,11... | collective-permute-start | bytes 786440 | tf_op jit(solution)/shard_map/ppermute | solution.py:256
  189.3 6.4 %collective-permute-done.other_ref = bf16[512,256]{1,0:T(8,128)(2,1)S(1)} collective-permute-done((bf16[512,256]{1,0:T(8,128)(2,1)S(1)}, bf16[512,256]{1,0:T(8,128)(2,1)S(1)}, u32[]{:S(2)}, u32[]{:S(2)}) %collective-permute-start) | collective-permute-done | bytes 262176 | tf_op jit(solution)/shard_map/ppermute | solution.py:256
  196.0 1.3 collective-permute-start.1
  197.4 1.0 collective-permute-done.1
  198.4 15.6 %all_to_all.33 = f32[64,1,640]{2,1,0:T(1,128)S(1)} all-to-all(f32[64,1,640]{2,1,0:T(1,128)S(1)} %bitcast.61), channel_id=1, replica_groups=mesh['z'=8,'y'=2,'x'=4,'core'=2,'col'=2] {'z','y','x'}, dimensions={0} | all-to-all | bytes 327680 | tf_op jit(solution)/shard_map/all_to_all | solution.py:15
  214.3 23.1 %all_to_all.34 = f32[128,1,640]{2,1,0:T(1,128)S(1)} all-to-all(f32[128,1,640]{2,1,0:T(1,128)S(1)} %broadcast_in_dim.7), channel_id=1, replica_groups=mesh['z'=8,'y'=2,'x'=4,'core'=2,'col'=2] {'col','z','y','x'}, dimensions={0} | all-to-all | bytes 655360 | tf_op jit(solution)/shard_map/all_to_all | solution.py:15
  237.4 3.3 %collective-permute-start.2 = (f32[128,1,640]{2,1,0:T(1,128)S(1)}, f32[128,1,640]{2,1,0:T(1,128)S(1)}, u32[]{:S(2)}, u32[]{:S(2)}) collective-permute-start(f32[128,1,640]{2,1,0:T(1,128)S(1)} %all_to_all.34), channel_id=1, source_target_pairs={{0,2},{2,0},{1,3},{3,1},{4,6},{6,4},{5,7},{7,5},{8,10},{10,8},{9,1... | collective-permute-start | bytes 983048 | tf_op jit(solution)/shard_map/ppermute | solution.py:262
  240.6 1.3 collective-permute-done.2
  241.9 18.0 %shard_map.65 = f32[512,256]{1,0:T(8,128)} custom-call(s32[1]{0:T(128)} %bitcast.side_ref, s32[1]{0:T(128)} %bitcast.1.core_ref, f32[640,128]{1,0:T(8,128)S(1)} %bitcast.44, f32[640,128]{1,0:T(8,128)S(1)} %bitcast.45, bf16[512,256]{1,0:T(8,128)(2,1)S(1)} %convolution_convert_fusion.3.mine_ref, bf16[512,256]{1,0:T(8,128)(2,1)S(1)} %collective-permute-done.other_ref), custom_call_target="tpu_custom_call" | custom-call | tf_op jit(solution)/shard_map/pallas_call | solution.py:157
  (23 shorter events, 1.7 us)
Async XLA Ops:
  0.0 20.2 %copy-start.2 = (bf16[24,128,128]{2,1,0:T(8,128)(2,1)S(1)}, bf16[24,128,128]{2,1,0:T(8,128)(2,1)}, u32[]{:S(2)}) copy-start(bf16[24,128,128]{2,1,0:T(8,128)(2,1)} %param.6) | copy-start | bytes 2359300
  0.0 20.6 %copy-start.3 = (s32[24]{0:T(128)S(1)}, s32[24]{0:T(128)}, u32[]{:S(2)}) copy-start(s32[24]{0:T(128)} %param.7) | copy-start | bytes 292
  5.4 30.5 %all-to-all-start = ((bf16[128,2,640]{2,1,0:T(2,128)(2,1)}), bf16[128,2,640]{2,1,0:T(2,128)(2,1)S(1)}, u32[]{:S(2)}, u32[]{:S(2)}) async-start(bf16[128,2,640]{2,1,0:T(2,128)(2,1)} %copy.19), calls=%async_computation | async-start | bytes 655360 | tf_op jit(solution)/shard_map/all_to_all | solution.py:15
  22.9 65.1 %copy-start = (bf16[384,8,4,128]{3,1,2,0:T(8,128)(2,1)}, bf16[384,8,4,128]{3,1,2,0:T(8,128)(2,1)S(1)}, u32[]{:S(2)}) copy-start(bf16[384,8,4,128]{3,1,2,0:T(8,128)(2,1)S(1)} %copy.26) | copy-start | bytes 9437188
  138.3 47.3 %copy-start.1 = (bf16[384,8,4,128]{3,1,2,0:T(8,128)(2,1)S(1)}, bf16[384,8,4,128]{3,1,2,0:T(8,128)(2,1)}, u32[]{:S(2)}) copy-start(bf16[384,8,4,128]{3,1,2,0:T(8,128)(2,1)} %copy-done) | copy-start | bytes 9437188
  186.6 9.1 %collective-permute-start = (bf16[512,256]{1,0:T(8,128)(2,1)S(1)}, bf16[512,256]{1,0:T(8,128)(2,1)S(1)}, u32[]{:S(2)}, u32[]{:S(2)}) collective-permute-start(bf16[512,256]{1,0:T(8,128)(2,1)S(1)} %convolution_convert_fusion.3.mine_ref), channel_id=1, source_target_pairs={{0,1},{1,0},{2,3},{3,2},{4,5},{5,4},{6,7},{7,6},{8,9},{9,8},{10,11... | collective-permute-start | bytes 786440 | tf_op jit(solution)/shard_map/ppermute | solution.py:256
  196.0 2.4 collective-permute-start.1
  237.4 4.5 %collective-permute-start.2 = (f32[128,1,640]{2,1,0:T(1,128)S(1)}, f32[128,1,640]{2,1,0:T(1,128)S(1)}, u32[]{:S(2)}, u32[]{:S(2)}) collective-permute-start(f32[128,1,640]{2,1,0:T(1,128)S(1)} %all_to_all.34), channel_id=1, source_target_pairs={{0,2},{2,0},{1,3},{3,1},{4,6},{6,4},{5,7},{7,5},{8,10},{10,8},{9,1... | collective-permute-start | bytes 983048 | tf_op jit(solution)/shard_map/ppermute | solution.py:262

commit v5 on v4

--- a/solution.py
+++ b/solution.py
@@ -226,12 +226,13 @@
     wide = wide.reshape(edge * slots, RB_DEV * edge)
     kept = spread(packed, GROUPS)
     row_part = own_blocks // 2 * width
-    kept_rows = kept[:, :, :row_part].reshape(blocks, width)
+    kept_rows = kept[:, :, :row_part].reshape(owners, own_blocks, width)
+    kept_rows = jnp.swapaxes(kept_rows, 0, 1).reshape(blocks, width)
     kept_notes = kept[:, :, row_part:].reshape(owners, width).astype(f32)
-    kept_scale = kept_notes[:, :own_blocks].reshape(blocks, 1)
+    kept_scale = kept_notes[:, :own_blocks].T.reshape(blocks, 1)
     all_runs = kept_notes[:, own_blocks : own_blocks + slots]
     all_members = kept_notes[:, own_blocks + slots : own_blocks + 2 * slots]
-    all_cols = (all_runs * own_blocks + all_members).astype(jnp.int32)
+    all_cols = jnp.where(all_runs < 0, -1, all_members * owners + all_runs).astype(jnp.int32)
     block_ids = jnp.arange(blocks, dtype=jnp.int32)
     picks = (all_cols[:, :, None] == block_ids).astype(bf16).reshape(owners * slots, blocks)
     squared = kept_scale * kept_scale

time: 260 us -> 261 us (level)
  no operation moved by 1% of the time
where the time goes in v5:
time: 261 us
  blocking collectives  178 us (68%)
  starting transfers between devices  22.1 us (8%)
  waiting for transfers between devices  21.6 us (8%)
  Pallas kernels  18.3 us (7%)
  other arithmetic  7.34 us (3%)
  local copies, waits for them, and re-layouts  6.46 us (2%)
  matrix products  6.01 us (2%)
    all_to_all x5, blocking collectives, spread(): return lax.all_to_all(rows, axes, split_axis=0, concat_axis=0, tiled=True)  178 us
    pallas_call x1, Pallas kernels, basis(): pl.pallas_call(basis_body, out_shape=jax.ShapeDtypeStruct(mine.shape, F32...  18 us
    all_to_all x1, starting transfers between devices, spread(): return lax.all_to_all(rows, axes, split_axis=0, concat_axis=0, tiled=True)  14.8 us
    all_to_all x1, waiting for transfers between devices, spread(): return lax.all_to_all(rows, axes, split_axis=0, concat_axis=0, tiled=True)  12.9 us
    ppermute x1, waiting for transfers between devices, local(): other = lax.ppermute(power_rows, 'col', [(0, 1), (1, 0)])  6.35 us
  transfers between devices with their start and end apart: 4, of which 4 were waited for; matrix products, arithmetic and copies ran while one was open for 1% of the time, Pallas kernels for 0%

profile of v5, /device:TPU:1, one launch (start us, length us, event | category | flops | bytes accessed | tf_op | source)
XLA Modules:
  0.0 260.8 jit_solution(9535282105362501316)
XLA Ops:
  0.7 0.7 convert_element_type.57
  1.4 1.1 multiply_convert_fusion
  2.7 0.7 fusion.6
  3.4 0.8 pad_maximum_fusion.1
  4.2 1.2 copy.21
  5.4 14.8 %all-to-all-start = ((bf16[128,2,640]{2,1,0:T(2,128)(2,1)}), bf16[128,2,640]{2,1,0:T(2,128)(2,1)S(1)}, u32[]{:S(2)}, u32[]{:S(2)}) async-start(bf16[128,2,640]{2,1,0:T(2,128)(2,1)} %copy.21), calls=%async_computation | async-start | bytes 655360 | tf_op jit(solution)/shard_map/all_to_all | solution.py:15
  20.7 1.7 broadcast_multiply_fusion
  22.9 12.9 %all-to-all-done = bf16[128,2,640]{2,1,0:T(2,128)(2,1)S(1)} async-done(((bf16[128,2,640]{2,1,0:T(2,128)(2,1)}), bf16[128,2,640]{2,1,0:T(2,128)(2,1)S(1)}, u32[]{:S(2)}, u32[]{:S(2)}) %all-to-all-start) | async-done | bytes 327712 | tf_op jit(solution)/shard_map/all_to_all | solution.py:15
  36.1 0.6 slice_multiply_fusion
  36.7 0.9 slice.24
  37.6 1.1 copy.28
  38.7 0.9 copy.25
  39.6 0.9 copy.31
  40.6 1.4 fusion
  42.0 1.0 convolution_convert_fusion.2
  43.0 44.9 %all_to_all.30 = bf16[128,24,256]{2,1,0:T(8,128)(2,1)S(1)} all-to-all(bf16[128,24,256]{2,1,0:T(8,128)(2,1)S(1)} %bitcast.61), channel_id=1, replica_groups=mesh['z'=8,'y'=2,'x'=4,'core'=2,'col'=2] {'z','y','x','core'}, dimensions={0} | all-to-all | bytes 3145728 | tf_op jit(solution)/shard_map/all_to_all | solution.py:15
  87.9 1.0 convolution_convert_fusion.4
  88.9 1.0 convolution_convert_fusion.1
  89.9 47.2 %all_to_all.31 = bf16[128,24,256]{2,1,0:T(8,128)(2,1)S(1)} all-to-all(bf16[128,24,256]{2,1,0:T(8,128)(2,1)S(1)} %bitcast.62), channel_id=1, replica_groups=mesh['z'=8,'y'=2,'x'=4,'core'=2,'col'=2] {'z','y','x','core'}, dimensions={0} | all-to-all | bytes 3145728 | tf_op jit(solution)/shard_map/all_to_all | solution.py:15
  137.1 1.0 fusion.1
  138.2 1.0 convolution_convert_fusion
  139.2 47.3 %all_to_all.32 = bf16[128,24,256]{2,1,0:T(8,128)(2,1)S(1)} all-to-all(bf16[128,24,256]{2,1,0:T(8,128)(2,1)S(1)} %bitcast.60), channel_id=1, replica_groups=mesh['z'=8,'y'=2,'x'=4,'core'=2,'col'=2] {'z','y','x','core'}, dimensions={0} | all-to-all | bytes 3145728 | tf_op jit(solution)/shard_map/all_to_all | solution.py:15
  186.5 1.0 convolution_convert_fusion.3.mine_ref
  187.5 2.7 %collective-permute-start = (bf16[512,256]{1,0:T(8,128)(2,1)S(1)}, bf16[512,256]{1,0:T(8,128)(2,1)S(1)}, u32[]{:S(2)}, u32[]{:S(2)}) collective-permute-start(bf16[512,256]{1,0:T(8,128)(2,1)S(1)} %convolution_convert_fusion.3.mine_ref), channel_id=1, source_target_pairs={{0,1},{1,0},{2,3},{3,2},{4,5},{5,4},{6,7},{7,6},{8,9},{9,8},{10,11... | collective-permute-start | bytes 786440 | tf_op jit(solution)/shard_map/ppermute | solution.py:257
  190.2 6.4 %collective-permute-done.other_ref = bf16[512,256]{1,0:T(8,128)(2,1)S(1)} collective-permute-done((bf16[512,256]{1,0:T(8,128)(2,1)S(1)}, bf16[512,256]{1,0:T(8,128)(2,1)S(1)}, u32[]{:S(2)}, u32[]{:S(2)}) %collective-permute-start) | collective-permute-done | bytes 262176 | tf_op jit(solution)/shard_map/ppermute | solution.py:257
  196.9 1.3 collective-permute-start.1
  198.3 1.0 collective-permute-done.1
  199.3 15.6 %all_to_all.33 = f32[64,1,640]{2,1,0:T(1,128)S(1)} all-to-all(f32[64,1,640]{2,1,0:T(1,128)S(1)} %bitcast.69), channel_id=1, replica_groups=mesh['z'=8,'y'=2,'x'=4,'core'=2,'col'=2] {'z','y','x'}, dimensions={0} | all-to-all | bytes 327680 | tf_op jit(solution)/shard_map/all_to_all | solution.py:15
  215.2 23.1 %all_to_all.34 = f32[128,1,640]{2,1,0:T(1,128)S(1)} all-to-all(f32[128,1,640]{2,1,0:T(1,128)S(1)} %broadcast_in_dim.12), channel_id=1, replica_groups=mesh['z'=8,'y'=2,'x'=4,'core'=2,'col'=2] {'col','z','y','x'}, dimensions={0} | all-to-all | bytes 655360 | tf_op jit(solution)/shard_map/all_to_all | solution.py:15
  238.3 3.3 %collective-permute-start.2 = (f32[128,1,640]{2,1,0:T(1,128)S(1)}, f32[128,1,640]{2,1,0:T(1,128)S(1)}, u32[]{:S(2)}, u32[]{:S(2)}) collective-permute-start(f32[128,1,640]{2,1,0:T(1,128)S(1)} %all_to_all.34), channel_id=1, source_target_pairs={{0,2},{2,0},{1,3},{3,1},{4,6},{6,4},{5,7},{7,5},{8,10},{10,8},{9,1... | collective-permute-start | bytes 983048 | tf_op jit(solution)/shard_map/ppermute | solution.py:263
  241.5 1.3 collective-permute-done.2
  242.8 18.0 %shard_map.65 = f32[512,256]{1,0:T(8,128)} custom-call(s32[1]{0:T(128)} %bitcast.side_ref, s32[1]{0:T(128)} %bitcast.1.core_ref, f32[640,128]{1,0:T(8,128)S(1)} %bitcast.51, f32[640,128]{1,0:T(8,128)S(1)} %bitcast.52, bf16[512,256]{1,0:T(8,128)(2,1)S(1)} %convolution_convert_fusion.3.mine_ref, bf16[512,256]{1,0:T(8,128)(2,1)S(1)} %collective-permute-done.other_ref), custom_call_target="tpu_custom_call" | custom-call | tf_op jit(solution)/shard_map/pallas_call | solution.py:157
  (26 shorter events, 2.3 us)
Async XLA Ops:
  0.0 20.2 %copy-start.2 = (bf16[24,128,128]{2,1,0:T(8,128)(2,1)S(1)}, bf16[24,128,128]{2,1,0:T(8,128)(2,1)}, u32[]{:S(2)}) copy-start(bf16[24,128,128]{2,1,0:T(8,128)(2,1)} %param.6) | copy-start | bytes 2359300
  0.0 20.6 %copy-start.4 = (s32[24]{0:T(128)S(1)}, s32[24]{0:T(128)}, u32[]{:S(2)}) copy-start(s32[24]{0:T(128)} %param.7) | copy-start | bytes 292
  5.4 30.5 %all-to-all-start = ((bf16[128,2,640]{2,1,0:T(2,128)(2,1)}), bf16[128,2,640]{2,1,0:T(2,128)(2,1)S(1)}, u32[]{:S(2)}, u32[]{:S(2)}) async-start(bf16[128,2,640]{2,1,0:T(2,128)(2,1)} %copy.21), calls=%async_computation | async-start | bytes 655360 | tf_op jit(solution)/shard_map/all_to_all | solution.py:15
  22.9 66.0 %copy-start = (bf16[384,8,4,128]{3,1,2,0:T(8,128)(2,1)}, bf16[384,8,4,128]{3,1,2,0:T(8,128)(2,1)S(1)}, u32[]{:S(2)}) copy-start(bf16[384,8,4,128]{3,1,2,0:T(8,128)(2,1)S(1)} %copy.34) | copy-start | bytes 9437188
  39.6 2.5 copy-start.3
  139.2 47.3 %copy-start.1 = (bf16[384,8,4,128]{3,1,2,0:T(8,128)(2,1)S(1)}, bf16[384,8,4,128]{3,1,2,0:T(8,128)(2,1)}, u32[]{:S(2)}) copy-start(bf16[384,8,4,128]{3,1,2,0:T(8,128)(2,1)} %copy-done) | copy-start | bytes 9437188
  187.5 9.1 %collective-permute-start = (bf16[512,256]{1,0:T(8,128)(2,1)S(1)}, bf16[512,256]{1,0:T(8,128)(2,1)S(1)}, u32[]{:S(2)}, u32[]{:S(2)}) collective-permute-start(bf16[512,256]{1,0:T(8,128)(2,1)S(1)} %convolution_convert_fusion.3.mine_ref), channel_id=1, source_target_pairs={{0,1},{1,0},{2,3},{3,2},{4,5},{5,4},{6,7},{7,6},{8,9},{9,8},{10,11... | collective-permute-start | bytes 786440 | tf_op jit(solution)/shard_map/ppermute | solution.py:257
  196.9 2.4 collective-permute-start.1
  238.3 4.5 %collective-permute-start.2 = (f32[128,1,640]{2,1,0:T(1,128)S(1)}, f32[128,1,640]{2,1,0:T(1,128)S(1)}, u32[]{:S(2)}, u32[]{:S(2)}) collective-permute-start(f32[128,1,640]{2,1,0:T(1,128)S(1)} %all_to_all.34), channel_id=1, source_target_pairs={{0,2},{2,0},{1,3},{3,1},{4,6},{6,4},{5,7},{7,5},{8,10},{10,8},{9,1... | collective-permute-start | bytes 983048 | tf_op jit(solution)/shard_map/ppermute | solution.py:263
